TPU v7x, 32 devices: a whole 2x2x4 slice. The times are simulated.
32 devices in a mesh: row: 4 (over y, core), blk: 8 (over z, x).
Axes of the slice: x: 2, y: 2, z: 4, core: 2. Of those that a mesh axis runs over, the one named last changes fastest.
Arguments:
- theta: float32 [8, 8, 256, 256], P('blk'), may hold values from -6 to 6
- left_env: float32 [16, 8, 256, 256], P('row', 'blk'), may hold values from -0.375 to 0.375
- right_env: float32 [16, 8, 256, 256], P('row', 'blk'), may hold values from -0.375 to 0.375
- left_tiles: int32 [8], replicated, may hold values from 1 to 4
- right_tiles: int32 [8], replicated, may hold values from 1 to 4
- pairs: int32 [48, 2], replicated, may hold values from 0 to 15
- coefs: float32 [48], replicated, may hold values from -2 to 2
Outputs:
- hpsi: float32 [8, 8, 256, 256], P('blk', None, 'row')
All inputs are finite; a program needn't handle non-finite values.
Results may differ from a plain program's by a relative error of at most 0.000071.
Values sent between devices are 32-bit elements; how exact they have to be, the bound alone decides.
No kernel may reach another device: no remote copies, remote signals or barrier semaphores. Data moves between devices by JAX's collectives and lax.ppermute only.
A program may use at most 128 MiB of HBM per device.

v0:
```python
import jax
import jax.numpy as jnp
from jax import lax
from jax.sharding import PartitionSpec as P


def per_device(theta, left_env, right_env, left_tiles, right_tiles, pairs, coefs):
    bond_local = left_env.shape[0]
    bond_total = bond_local * lax.axis_size("row")
    left_count = theta.shape[0]
    block_rows = theta.shape[2]
    row_parts = lax.axis_size("row")
    row_at = lax.axis_index("row")
    blk_at = lax.axis_index("blk")
    quarter = block_rows // 4
    cells = jnp.arange(block_rows)
    tiles_here = lax.dynamic_slice_in_dim(left_tiles, blk_at * left_count, left_count, 0)
    left_mask = (cells[None, :] < quarter * tiles_here[:, None]).astype(jnp.float32)
    right_mask = (cells[None, :] < quarter * right_tiles[:, None]).astype(jnp.float32)
    masked = theta * left_mask[:, None, :, None] * right_mask[None, :, None, :]
    bonds = jnp.arange(bond_total)
    onehot_left = (pairs[:, 0][:, None] == bonds[None, :]).astype(jnp.float32)
    onehot_right = (pairs[:, 1][:, None] == bonds[None, :]).astype(jnp.float32)
    couplings = jnp.einsum(
        "ka,kb->ab", onehot_left * coefs[:, None], onehot_right, precision=lax.Precision.HIGHEST
    )
    couple_local = lax.dynamic_slice_in_dim(couplings, row_at * bond_local, bond_local, 1)
    dressed = lax.psum_scatter(
        jnp.einsum("ab,bqij->aqij", couple_local, right_env, precision=lax.Precision.HIGHEST),
        "row",
        scatter_dimension=0,
        tiled=True,
    )
    slab = block_rows // row_parts
    row_ids = row_at * slab + jnp.arange(slab)
    out_left = (row_ids[None, :] < quarter * tiles_here[:, None]).astype(jnp.float32)
    partial_value = jnp.einsum(
        "apij,pqjk->apqik", left_env, masked, precision=lax.Precision.HIGHEST
    )
    summed = jnp.einsum(
        "apqik,aqlk->pqil",
        partial_value,
        lax.all_gather(dressed, "blk", axis=1, tiled=True),
        precision=lax.Precision.HIGHEST,
    )
    result = lax.psum_scatter(summed, "row", scatter_dimension=2, tiled=True)
    return result * out_left[:, None, :, None] * right_mask[None, :, None, :]


def solution(mesh):
    return jax.shard_map(
        per_device,
        mesh=mesh,
        in_specs=(
            P("blk", None, None, None),
            P("row", "blk", None, None),
            P("row", "blk", None, None),
            P(),
            P(),
            P(),
            P(),
        ),
        out_specs=P("blk", None, "row", None),
        check_vma=False,
    )
```

profile of v0, /device:TPU:0, one launch (start us, length us, event | category | flops | bytes accessed | tf_op | source)
XLA Modules:
  0.0 243.7 jit_solution(2779027135037797493)
XLA Ops:
  6.5 0.0 copy-start
  6.5 0.0 reduce-scatter.3.cloned.1.call-start
  6.5 0.8 slice_bitcast_fusion.1
  7.3 0.9 fusion.13
  8.2 5.3 %convolution_bitcast_fusion = f32[16,1,256,256]{3,0,2,1:T(8,128)S(1)} fusion(f32[4,256,256]{2,1,0:T(8,128)} %bitcast.39, f32[16,16]{0,1:T(8,128)S(1)} %fusion.13, s32[]{:T(128)S(6)} %select_n.6), kind=kOutput, calls=%fused_computation.2 | convolution fusion | flops 50331648 | bytes 5244932 | tf_op jit(solution)/shard_map/ab,bqij->aqij/dot_general | solution.py:29
  13.6 4.4 %copy.14 = f32[16,1,256,256]{3,2,1,0:T(8,128)} copy(f32[16,1,256,256]{3,0,2,1:T(8,128)S(1)} %convolution_bitcast_fusion) | data formatting | bytes 8388608 | tf_op jit(solution)/shard_map/ab,bqij->aqij/dot_general | solution.py:29
  17.9 0.0 reduce-scatter.3.cloned.1.call-update
  18.0 0.0 all-gather.2.cloned.1.call-start
  18.0 47.4 %reduce-scatter.3.cloned.1.call-done = f32[4,1,256,256]{3,2,1,0:T(8,128)} async-done(((f32[16,1,256,256]{3,2,1,0:T(8,128)}), f32[4,1,256,256]{3,2,1,0:T(8,128)}) %reduce-scatter.3.cloned.1.call-update) | async-done | bytes 1048592 | tf_op jit(solution)/shard_map/reduce_scatter | solution.py:28
  65.4 0.0 all-gather.2.cloned.1.call-update
  65.4 0.2 reduce-scatter.5.cloned.1.call-start
  65.7 0.0 copy-done.2
  65.7 0.6 dynamic_slice.7
  66.9 0.0 copy-done.3
  66.9 0.1 fusion.19
  67.0 0.0 copy-done
  67.0 15.5 %fusion.2 = f32[8,256,4,256]{3,1,2,0:T(8,128)} fusion(f32[1,8,256,256]{3,2,1,0:T(8,128)S(1)} %copy-done.1, f32[4,1,256,256]{3,2,1,0:T(8,128)S(1)} %copy-done, f32[8,256]{1,0:T(8,128)S(1)} %fusion.19, f32[256]{0:T(256)S(1)} %compare_convert_fusion.1), kind=kOutput, calls=%fused_computation.3 | convolution fusion | flops 6443499520 | bytes 11543552 | tf_op jit(solution)/shard_map/apij,pqjk->apqik/dot_general | solution.py:37
  82.5 109.5 %all-gather.2.cloned.1.call-done = f32[4,8,256,256]{3,2,0,1:T(8,128)} async-done(((f32[4,1,256,256]{3,2,0,1:T(8,128)}), f32[4,8,256,256]{3,2,0,1:T(8,128)}) %all-gather.2.cloned.1.call-update) | async-done | bytes 8388624 | tf_op jit(solution)/shard_map/all_gather | solution.py:43
  192.0 11.4 %fusion.6 = f32[1,8,256,256]{2,3,1,0:T(8,128)S(1)} fusion(f32[4,8,256,256]{3,2,0,1:T(8,128)} %all-gather.2.cloned.1.call-done, f32[8,256,4,256]{3,1,2,0:T(8,128)} %fusion.2), kind=kOutput, calls=%fused_computation.7 | convolution fusion | flops 6442450944 | bytes 18874368 | tf_op jit(solution)/shard_map/apqik,aqlk->pqil/dot_general | solution.py:40
  203.4 2.0 copy.18
  205.5 0.0 reduce-scatter.5.cloned.1.call-update
  205.5 29.5 %reduce-scatter.5.cloned.1.call-done = f32[1,8,64,256]{3,1,0,2:T(8,128)} async-done(((f32[1,8,256,256]{3,1,0,2:T(8,128)}), f32[1,8,64,256]{3,1,0,2:T(8,128)}) %reduce-scatter.5.cloned.1.call-update) | async-done | bytes 524304 | tf_op jit(solution)/shard_map/reduce_scatter | solution.py:46
  235.0 1.2 multiply_multiply_fusion
  236.2 1.0 copy.19
  (7 shorter events, 0.0 us)
Async XLA Ops:
  6.5 60.5 %copy-start = (f32[4,1,256,256]{3,2,1,0:T(8,128)S(1)}, f32[4,1,256,256]{3,2,1,0:T(8,128)}, u32[]{:S(2)}) copy-start(f32[4,1,256,256]{3,2,1,0:T(8,128)} %param.8) | copy-start | bytes 3145732
  6.5 58.9 %reduce-scatter.3.cloned.1.call-start = ((), (), s32[]{:S(2)}) async-start(), calls=%async_computation.2 | async-start | bytes 5242880 | tf_op jit(solution)/shard_map/reduce_scatter | solution.py:28
  17.9 47.7 %copy-start.2 = (s32[8]{0:T(128)S(1)}, s32[8]{0:T(128)}, u32[]{:S(2)}) copy-start(s32[8]{0:T(128)} %param.10) | copy-start | bytes 100
  17.9 49.0 %copy-start.3 = (s32[8]{0:T(128)S(1)}, s32[8]{0:T(128)}, u32[]{:S(2)}) copy-start(s32[8]{0:T(128)} %param.11) | copy-start | bytes 100
  17.9 49.1 %copy-start.1 = (f32[1,8,256,256]{3,2,1,0:T(8,128)S(1)}, f32[1,8,256,256]{3,2,1,0:T(8,128)}, u32[]{:S(2)}) copy-start(f32[1,8,256,256]{3,2,1,0:T(8,128)} %param.7) | copy-start | bytes 6291460
  18.0 174.1 %all-gather.2.cloned.1.call-start = ((), (), s32[]{:S(2)}) async-start(), calls=%async_computation.3 | async-start | bytes 9437184 | tf_op jit(solution)/shard_map/all_gather | solution.py:43
  65.4 169.6 %reduce-scatter.5.cloned.1.call-start = ((), (), s32[]{:S(2)}) async-start(), calls=%async_computation.4 | async-start | bytes 2621440 | tf_op jit(solution)/shard_map/reduce_scatter | solution.py:46
Sparse Core Ops, SparseCore 0:
  18.1 47.2 reduce-scatter.2
  67.5 124.4 all-gather.1
  205.6 29.3 reduce-scatter.4
where the time goes:
time: 244 us
  waiting for transfers between devices  186 us (76%)
  matrix products  33.2 us (14%)
  between operations  13.8 us (6%)
  local copies, waits for them, and re-layouts  8.73 us (4%)
    all_gather x1, waiting for transfers between devices, per_device(): lax.all_gather(dressed, 'blk', axis=1, tiled=True)  109 us
    reduce_scatter x1, waiting for transfers between devices, per_device(): lax.psum_scatter(jnp.einsum('ab,bqij->aqij', couple_local, right_env, pre...  47.4 us
    reduce_scatter x1, waiting for transfers between devices, per_device(): result = lax.psum_scatter(summed, 'row', scatter_dimension=2, tiled=True)  29.5 us
    dot_general x1, matrix products, per_device(): jnp.einsum('apij,pqjk->apqik', left_env, masked, precision=lax.Precision....  15.5 us
    dot_general x1, matrix products, per_device(): jnp.einsum('apqik,aqlk->pqil', partial_value, lax.all_gather(dressed, 'bl...  11.4 us
    dot_general x1, matrix products, per_device(): jnp.einsum('ab,bqij->aqij', couple_local, right_env, precision=lax.Precis...  5.31 us
  transfers between devices with their start and end apart: 3, of which 3 were waited for; matrix products, arithmetic and copies ran while one was open for 7% of the time, Pallas kernels for 0%

commit v1 on v0

v1 whole, which is shorter than its diff:
```python
import functools

import jax
import jax.numpy as jnp
from jax import lax
from jax.experimental import pallas as pl
from jax.experimental.pallas import tpu as pltpu
from jax.sharding import PartitionSpec as P


F32 = jnp.float32
BF16 = jnp.bfloat16
VMEM = pl.BlockSpec(memory_space=pltpu.VMEM)
SMEM = pl.BlockSpec(memory_space=pltpu.SMEM)
ANY = pl.BlockSpec(memory_space=pl.ANY)


def split(value):
    high = value.astype(BF16)
    return high, (value - high.astype(F32)).astype(BF16)


def product(left, right, dims):
    def one(a, b):
        return lax.dot_general(a, b, (dims, ((), ())), preferred_element_type=F32)

    return one(left[0], right[0]) + (one(left[0], right[1]) + one(left[1], right[0]))


def dress_kernel(shifts, rows, info, couplings, *refs):
    parts, rest = refs[: len(shifts)], refs[len(shifts) :]
    outs, before = rest[-2:], rest[:-2]
    half = rows // 2
    row = info[0]
    count, size = outs[0].shape[0], outs[0].shape[2]
    slab = size // rows
    chunk = min(32, slab)
    factors = [
        [[couplings[(row ^ shift) * count + a, row * count + b] for b in range(count)] for a in range(count)]
        for shift in shifts
    ]
    for kind in range(2):
        for j in range(half):
            begin = (row ^ (2 * j + 1 - kind)) * slab
            for c in range(slab // chunk):
                at = pl.ds(pl.multiple_of(begin + c * chunk, chunk), chunk)
                to = pl.ds(j * slab + c * chunk, chunk)
                totals = [before[kind][b, to, :] if before else None for b in range(count)]
                for part, by in zip(parts, factors):
                    for a in range(count):
                        value = part[a, at, :]
                        for b in range(count):
                            term = by[a][b] * value
                            totals[b] = term if totals[b] is None else totals[b] + term
                for b in range(count):
                    outs[kind][b, to, :] = totals[b]


def dress(shifts, rows, info, couplings, parts, before=()):
    count, size, _ = parts[0].shape
    shape = jax.ShapeDtypeStruct((count, size // 2, size), F32)
    return pl.pallas_call(
        functools.partial(dress_kernel, shifts, rows),
        out_shape=[shape, shape],
        in_specs=[SMEM, SMEM] + [VMEM] * (len(parts) + len(before)),
        out_specs=[VMEM, VMEM],
        cost_estimate=pl.CostEstimate(
            flops=8 * parts[0].size * len(parts),
            bytes_accessed=4 * parts[0].size * (len(parts) + 2),
            transcendentals=0,
        ),
        name="dress",
    )(info, couplings, *parts, *before)


def pair_kernel(spec, info, left_tiles, right_tiles, *refs):
    rows, inner, n_in, jobs, kinds, slots = spec
    ins, outs = refs[:n_in], dict(zip(kinds, refs[n_in : n_in + len(kinds)]))
    held = refs[n_in + len(kinds) : -2]
    thetas, sem = refs[-2], refs[-1]
    row, high, low, x_at = info[0], info[1], info[2], info[3]
    size = thetas.shape[-1]
    quarter = size // 4
    width = size // 2
    count = 2 * inner
    slab = size // rows
    half = rows // 2

    def local_of(k, s):
        return ((high + k) % 2) * inner + (x_at + inner - s) % inner

    copies, theta_copies = {}, []
    for lefts, theta_at, relative, foreign, pieces in jobs:
        for i in [i for i, _ in lefts]:
            if i not in copies:
                copies[i] = pltpu.make_async_copy(ins[i], held[slots[i]], sem.at[i])
                copies[i].start()
        for k, s, _, rights in pieces:
            local = local_of(k, s)
            if relative:
                per = count // rows
                place = ((local // per) ^ row) * per + local % per
            else:
                place = low * count + local
            n = len(theta_copies)
            theta_copies.append(
                pltpu.make_async_copy(ins[theta_at].at[place], thetas.at[n], sem.at[n_in + n])
            )
            theta_copies[n].start()
            for i in rights:
                if i not in copies:
                    copies[i] = pltpu.make_async_copy(ins[i], held[slots[i]], sem.at[i])
                    copies[i].start()
    waited = set()

    def ready(i):
        if i not in waited:
            copies[i].wait()
            waited.add(i)
        return held[slots[i]]

    made = {kind: 0 for kind in kinds}
    n = 0
    for lefts, _, relative, foreign, pieces in jobs:
        tile = left_tiles[(2 * high + (1 - low if foreign else low)) * inner + x_at]
        depth = lax.broadcasted_iota(jnp.int32, (size, size), 0)
        wide = lax.broadcasted_iota(jnp.int32, (size, size), 1)
        for k, s, column, rights in pieces:
            limit = quarter * right_tiles[low * count + local_of(k, s)]
            left_refs = [ready(i) for i, _ in lefts]
            theta_copies[n].wait()
            inside = jnp.logical_and(depth < quarter * tile, wide < limit)
            masked = split(jnp.where(inside, thetas[n], 0.0))
            n += 1
            right_refs = [ready(i) for i in rights]
            part = left_refs[0].shape[1]
            columns = sum(r.shape[1] for r in right_refs)
            total = None
            for b in range(left_refs[0].shape[0]):
                left = left_refs[0][b]
                right = right_refs[0][b]
                if len(left_refs) > 1:
                    left = jnp.concatenate([r[b] for r in left_refs], axis=0)
                if len(right_refs) > 1:
                    right = jnp.concatenate([r[b] for r in right_refs], axis=0)
                partial_value = split(product(split(left), masked, ((1,), (0,))))
                term = product(partial_value, split(right), ((1,), (1,)))
                total = term if total is None else total + term
            in_right = lax.broadcasted_iota(jnp.int32, (slab, columns), 1) + column < limit
            at_row = lax.broadcasted_iota(jnp.int32, (slab, columns), 0)
            for at, (_, kind) in enumerate(lefts):
                for j in range(half):
                    shift = 2 * j + 1 if kind == "send" else 2 * j
                    begin = at * part + j * slab
                    value = jnp.where(
                        jnp.logical_and(in_right, at_row + (row ^ shift) * slab < quarter * tile),
                        total[begin : begin + slab],
                        0.0,
                    )
                    for w in range(columns // width):
                        outs[kind][j, made[kind] + w] = value[:, w * width : (w + 1) * width]
                made[kind] += columns // width
    assert len(waited) == len(copies)


def pair_products(rows, inner, scalars, jobs):
    arrays = []

    def index(array):
        for i, known in enumerate(arrays):
            if known is array:
                return i
        arrays.append(array)
        return len(arrays) - 1

    compact, streamed = [], []
    units = {}
    flops, n_thetas = 0, 0
    size = jobs[0][1].shape[-1]
    for lefts, theta, relative, foreign, pieces in jobs:
        lefts_at = tuple((index(a), kind) for a, kind in lefts)
        pieces_at = tuple((k, s, c, tuple(index(r) for r in rights)) for k, s, c, rights in pieces)
        compact.append((lefts_at, index(theta), relative, foreign, pieces_at))
        streamed += [i for i, _ in lefts_at] + [i for piece in pieces_at for i in piece[3]]
        n_thetas += len(pieces)
        for _, kind in lefts:
            units[kind] = units.get(kind, 0) + sum(r.shape[1] for p in pieces for r in p[3]) // (size // 2)
        flops += 12 * len(lefts) * len(pieces) * lefts[0][0].size * size
    streamed = sorted(set(streamed))
    slots = {i: n for n, i in enumerate(streamed)}
    kinds = tuple(units)
    out = pl.pallas_call(
        functools.partial(pair_kernel, (rows, inner, len(arrays), tuple(compact), kinds, slots)),
        out_shape=[
            jax.ShapeDtypeStruct((rows // 2, units[kind], size // rows, size // 2), F32) for kind in kinds
        ],
        in_specs=[SMEM] * 3 + [ANY] * len(arrays),
        out_specs=[VMEM] * len(kinds),
        scratch_shapes=[pltpu.VMEM(arrays[i].shape, F32) for i in streamed]
        + [pltpu.VMEM((n_thetas, size, size), F32), pltpu.SemaphoreType.DMA((len(arrays) + n_thetas,))],
        cost_estimate=pl.CostEstimate(
            flops=flops, bytes_accessed=4 * sum(arrays[i].size for i in streamed), transcendentals=0
        ),
        name="pair",
    )(*scalars, *arrays)
    return dict(zip(kinds, out))


def finish_kernel(inner, units, info, *refs):
    out = refs[-1]
    high, low, x_at = info[1], info[2], info[3]
    count = 2 * inner
    at = 0
    for foreign, terms, listed in units:
        for u, (k, s, w) in enumerate(listed):
            local = ((high + k) % 2) * inner + (x_at + inner - s) % inner
            index = (1 - low if foreign else low) * count + local
            value = refs[at][u]
            for t in range(1, terms):
                value = value + refs[at + t][u]
            width = value.shape[1]
            out[0, index, :, w * width : (w + 1) * width] = value
        at += terms


def finish(inner, info, groups, slab, size):
    arrays = [a for _, terms, _ in groups for a in terms]
    units = tuple((foreign, len(terms), tuple(listed)) for foreign, terms, listed in groups)
    return pl.pallas_call(
        functools.partial(finish_kernel, inner, units),
        out_shape=jax.ShapeDtypeStruct((1, 4 * inner, slab, size), F32),
        in_specs=[SMEM] + [VMEM] * len(arrays),
        out_specs=VMEM,
        cost_estimate=pl.CostEstimate(
            flops=4 * inner * slab * size, bytes_accessed=16 * inner * slab * size * 2, transcendentals=0
        ),
        name="finish",
    )(info, *arrays)


def per_device(rows, blks, theta, left_env, right_env, left_tiles, right_tiles, pairs, coefs):
    bond_total = left_env.shape[0] * rows
    size = theta.shape[2]
    slab = size // rows
    inner = blks // 4
    count = 2 * inner
    row = lax.axis_index("row")
    blk = lax.axis_index("blk")
    high, low, x_at = blk // count, (blk // inner) % 2, blk % inner
    info = jnp.stack([row, high, low, x_at]).astype(jnp.int32)
    scalars = (info, left_tiles, right_tiles)

    def by_row(value, shift):
        return lax.ppermute(value, "row", [(r, r ^ shift) for r in range(rows)])

    def by_blk(value, target):
        moves = []
        for h in range(2):
            for l in range(2):
                for x in range(inner):
                    a, b, c = target(h, l, x)
                    if (a, b, c) != (h, l, x):
                        moves.append(((h * 2 + l) * inner + x, (a * 2 + b) * inner + c))
        return lax.ppermute(value, "blk", moves)

    def partner(h, l, x):
        return h, 1 - l, x

    def gather_inner(value):
        return [value] + [by_blk(value, lambda h, l, x, s=s: (h, l, (x + s) % inner)) for s in range(1, inner)]

    left, right = left_env[:, 0], right_env[:, 0]
    halves = lax.optimization_barrier((right[:, : size // 2], right[:, size // 2 :]))

    bits = []
    while 1 << len(bits) < rows:
        bits.append(1 << len(bits))
    far, far_order = [left], [0]
    for bit in reversed(bits[1:]):
        far += [by_row(part, bit) for part in far]
        far_order += [s ^ bit for s in far_order]
    near = [by_row(left, 1)]

    def second_of(h, l, x):
        return (l + 1) % 2, h, x

    def first_of(h, l, x):
        return l, h, x

    per = count // rows
    theta_other = lax.dynamic_slice_in_dim(theta[0], (1 - low) * count + row * per, per, 0)
    theta_parts = [by_blk(theta_other, partner)]
    theta_order = [0]

    second_a = by_blk(halves[0], second_of)

    bonds = jnp.arange(bond_total)
    onehot_left = (pairs[:, 0][:, None] == bonds[None, :]).astype(F32)
    onehot_right = (pairs[:, 1][:, None] == bonds[None, :]).astype(F32)
    couplings = jnp.einsum(
        "ka,kb->ab", onehot_left * coefs[:, None], onehot_right, precision=lax.Precision.HIGHEST
    )
    early = dress([0, 1], rows, info, couplings, [left] + near)

    second_b = by_blk(halves[1], second_of)
    second_xa = gather_inner(second_a)
    for bit in reversed(bits[1:]):
        theta_parts += [by_row(t, bit) for t in theta_parts]
        theta_order += [s ^ bit for s in theta_order]
    crossed = [by_row(part, 1) for part in far[1:]]
    shifts = far_order[1:] + [s ^ 1 for s in far_order[1:]]
    dressed = dress(shifts, rows, info, couplings, far[1:] + crossed, early)
    dressed_other = [by_blk(dressed[0], partner), by_blk(dressed[1], partner)]

    moved_a = by_blk(halves[0], first_of)
    first_a = jnp.where(high == low, halves[0], moved_a)
    second_xb = gather_inner(second_b)
    theta_cross = by_row(jnp.concatenate(theta_parts), 1)
    moved_b = by_blk(halves[1], first_of)
    first_b = jnp.where(high == low, halves[1], lax.optimization_barrier((moved_b, first_a))[0])
    first_xa = gather_inner(first_a)
    first_xb = gather_inner(first_b)
    whole = {}
    for n, s in enumerate(theta_order):
        whole[s] = theta_parts[n]
        whole[s ^ 1] = theta_cross[n * per : (n + 1) * per]
    thetas_other = jnp.concatenate([whole[s] for s in range(rows)])

    own = [(dressed[0], "send"), (dressed[1], "keep")]
    their = [(dressed_other[0], "send"), (dressed_other[1], "keep")]
    seconds = [(1, s, 0, [second_xa[s], second_xb[s]]) for s in range(inner)]
    firsts = [(0, 0, 0, [first_a, first_b])]
    own_firsts = firsts + [(0, s, 0, [first_xa[s]]) for s in range(1, inner)]
    own_lasts = [(0, s, size // 2, [first_xb[s]]) for s in range(1, inner)]
    their_lasts = [(0, s, 0, [first_xa[s], first_xb[s]]) for s in range(1, inner)]

    def pairs_of(*jobs):
        return pair_products(rows, inner, scalars, list(jobs))

    own1 = pairs_of((own, theta[0], False, False, seconds))
    own1_got = by_row(own1["send"], 1)
    for1 = pairs_of((their, thetas_other, True, True, seconds + firsts))
    for1_got = by_row(for1["send"], 1)
    own2 = pairs_of((own, theta[0], False, False, own_firsts))
    own2_got = by_row(own2["send"], 1)
    last = pairs_of((their, thetas_other, True, True, their_lasts), (own, theta[0], False, False, own_lasts))
    last_got = by_row(last["send"], 1)

    def over_rows(value):
        for bit in bits[1:]:
            kept, gone = value[0::2], value[1::2]
            got = by_row(gone, bit)
            if bit == bits[-1]:
                return kept[0], got[0]
            value = kept + got
        return value[0], jnp.zeros_like(value[0])

    their_kept, their_got = over_rows(for1["keep"] + for1_got)
    own_kept, own_got = over_rows(jnp.concatenate([own1["keep"] + own1_got, own2["keep"] + own2_got], axis=1))
    back = by_blk(their_kept + their_got, partner)
    last_kept, last_other = over_rows(last["keep"] + last_got)
    n_last = 2 * len(their_lasts)
    last_back = by_blk(last_kept[:n_last] + last_other[:n_last], partner)

    units = [(1, s, w) for s in range(inner) for w in range(2)] + [(0, 0, 0), (0, 0, 1)]
    own_units = units + [(0, s, 0) for s in range(1, inner)]
    groups = [
        (False, [own_kept, own_got], own_units),
        (False, [last_kept[n_last:], last_other[n_last:]], [(0, s, 1) for s in range(1, inner)]),
        (True, [back], units),
        (True, [last_back], [(0, s, w) for s in range(1, inner) for w in range(2)]),
    ]
    return finish(inner, info, groups, slab, size)


def solution(mesh):
    def body(*args):
        return per_device(mesh.shape["row"], mesh.shape["blk"], *args)

    return jax.shard_map(
        body,
        mesh=mesh,
        in_specs=(
            P("blk", None, None, None),
            P("row", "blk", None, None),
            P("row", "blk", None, None),
            P(),
            P(),
            P(),
            P(),
        ),
        out_specs=P("blk", None, "row", None),
        check_vma=False,
    )
```

time: 244 us -> 141 us (0.58)
  waiting for transfers between devices: 186 us -> 39.9 us
  starting transfers between devices: 0.26 us -> 55.2 us
  Pallas kernels: 0 us -> 32.4 us
  matrix products: 33.2 us -> 0.86 us
  between operations: 13.8 us -> 0.26 us
  other arithmetic: 1.26 us -> 5.26 us
    all_gather x1 -> x0, waiting for transfers between devices: 109 us -> none  [per_device(): lax.all_gather(dressed, 'blk', axis=1, tiled=True)]
    reduce_scatter x2 -> x0, waiting for transfers between devices: 76.9 us -> none  [the longest x1 47.4 us: per_device(): lax.psum_scatter(jnp.einsum('ab,bqij->aqij', couple_local, right_env, pre...]
    ppermute x0 -> x25, starting transfers between devices: none -> 55.2 us  [the longest x13 46.8 us: by_blk(): return lax.ppermute(value, 'blk', moves)]
    ppermute x0 -> x25, waiting for transfers between devices: none -> 39.9 us  [the longest x13 21.5 us: by_blk(): return lax.ppermute(value, 'blk', moves)]
    pallas_call x0 -> x7, Pallas kernels: none -> 32.4 us  [the longest x4 24 us: pair_products(): pl.pallas_call(functools.partial(pair_kernel, (rows, inner, len(arrays),...]
    dot_general x3 -> x0, matrix products: 32.2 us -> none  [the longest x1 15.5 us: per_device(): jnp.einsum('apij,pqjk->apqik', left_env, masked, precision=lax.Precision....]
    dot_general x1 -> x0, local copies, waits for them, and re-layouts: 4.37 us -> none  [per_device(): jnp.einsum('ab,bqij->aqij', couple_local, right_env, precision=lax.Precis...]
    slice x0 -> x6, local copies, waits for them, and re-layouts: none -> 3.59 us  [the longest x1 1.3 us: per_device(): right[:, size // 2:]]
  transfers between devices with their start and end apart: 3 -> 25, of which waited for: 3 -> 8; matrix products, arithmetic and copies ran while one was open for 7% -> 8% of each run, Pallas kernels for 0% -> 22%
where the time goes in v1:
time: 141 us
  starting transfers between devices  55.2 us (39%)
  waiting for transfers between devices  39.9 us (28%)
  Pallas kernels  32.4 us (23%)
  local copies, waits for them, and re-layouts  7.17 us (5%)
  other arithmetic  5.26 us (4%)
    ppermute x13, starting transfers between devices, by_blk(): return lax.ppermute(value, 'blk', moves)  46.8 us
    pallas_call x4, Pallas kernels, pair_products(): pl.pallas_call(functools.partial(pair_kernel, (rows, inner, len(arrays),...  24 us
    ppermute x13, waiting for transfers between devices, by_blk(): return lax.ppermute(value, 'blk', moves)  21.5 us
    ppermute x12, waiting for transfers between devices, by_row(): return lax.ppermute(value, 'row', [(r, r ^ shift) for r in range(rows)])  18.4 us
    ppermute x12, starting transfers between devices, by_row(): return lax.ppermute(value, 'row', [(r, r ^ shift) for r in range(rows)])  8.36 us
    pallas_call x2, Pallas kernels, dress(): pl.pallas_call(functools.partial(dress_kernel, shifts, rows), out_shape=[...  6.27 us
  transfers between devices with their start and end apart: 25, of which 8 were waited for; matrix products, arithmetic and copies ran while one was open for 8% of the time, Pallas kernels for 22%

profile of v1, /device:TPU:0, one launch (start us, length us, event | category | flops | bytes accessed | tf_op | source)
XLA Modules:
  0.0 141.0 jit_solution(2494655384153766359)
XLA Ops:
  0.0 3.1 %collective-permute-start = (f32[4,256,256]{2,1,0:T(8,128)}, f32[4,256,256]{2,1,0:T(8,128)}, u32[]{:S(2)}, u32[]{:S(2)}) collective-permute-start(f32[4,256,256]{2,1,0:T(8,128)} %bitcast.27), channel_id=1, source_target_pairs={{0,16},{8,24},{16,0},{24,8},{1,17},{9,25},{17,1},{25,9},{2,18},{10... | collective-permute-start | bytes 3145736 | tf_op jit(solution)/shard_map/ppermute | solution.py:254
  6.8 3.7 %collective-permute-start.16 = (f32[1,256,256]{2,1,0:T(8,128)S(1)}, f32[1,256,256]{2,1,0:T(8,128)S(1)}, u32[]{:S(2)}, u32[]{:S(2)}) collective-permute-start(f32[1,256,256]{2,1,0:T(8,128)S(1)} %dynamic-slice_bitcast_fusion), channel_id=1, source_target_pairs={{0,2},{1,3},{2,0},{3,1},{4,6},{5,7},{6,4},{7,5},{8,10},{9,11},{10,... | collective-permute-start | bytes 786440 | tf_op jit(solution)/shard_map/ppermute | solution.py:264
  10.5 5.7 %collective-permute-done.16 = f32[1,256,256]{2,1,0:T(8,128)S(1)} collective-permute-done((f32[1,256,256]{2,1,0:T(8,128)S(1)}, f32[1,256,256]{2,1,0:T(8,128)S(1)}, u32[]{:S(2)}, u32[]{:S(2)}) %collective-permute-start.16) | collective-permute-done | bytes 262176 | tf_op jit(solution)/shard_map/ppermute | solution.py:264
  16.8 1.6 %collective-permute-start.3 = (f32[4,128,256]{2,1,0:T(8,128)S(1)}, f32[4,128,256]{2,1,0:T(8,128)}, u32[]{:S(2)}, u32[]{:S(2)}) collective-permute-start(f32[4,128,256]{2,1,0:T(8,128)S(1)} %get-tuple-element.24), channel_id=1, source_target_pairs={{0,4},{1,5},{2,0},{3,1},{4,6},{5,7},{6,2},{7,3},{8,12},{9,13},{10,... | collective-permute-start | bytes 1572872 | tf_op jit(solution)/shard_map/ppermute | solution.py:264
  19.9 7.5 %collective-permute-done.refs_0_ = f32[4,256,256]{2,1,0:T(8,128)} collective-permute-done((f32[4,256,256]{2,1,0:T(8,128)}, f32[4,256,256]{2,1,0:T(8,128)}, u32[]{:S(2)}, u32[]{:S(2)}) %collective-permute-start) | collective-permute-done | bytes 1048608 | tf_op jit(solution)/shard_map/ppermute | solution.py:254
  27.4 4.6 %collective-permute-done.17 = f32[1,256,256]{2,1,0:T(8,128)S(1)} collective-permute-done((f32[1,256,256]{2,1,0:T(8,128)S(1)}, f32[1,256,256]{2,1,0:T(8,128)S(1)}, u32[]{:S(2)}, u32[]{:S(2)}) %collective-permute-start.17) | collective-permute-done | bytes 262176 | tf_op jit(solution)/shard_map/ppermute | solution.py:254
  32.8 2.8 %collective-permute-start.4 = (f32[4,128,256]{2,1,0:T(8,128)S(1)}, f32[4,128,256]{2,1,0:T(8,128)}, u32[]{:S(2)}, u32[]{:S(2)}) collective-permute-start(f32[4,128,256]{2,1,0:T(8,128)S(1)} %get-tuple-element.25), channel_id=1, source_target_pairs={{0,4},{1,5},{2,0},{3,1},{4,6},{5,7},{6,2},{7,3},{8,12},{9,13},{10,... | collective-permute-start | bytes 1572872 | tf_op jit(solution)/shard_map/ppermute | solution.py:264
  37.0 1.8 %pad_maximum_fusion.1 = f32[2,256,256]{2,1,0:T(8,128)} fusion(f32[1,256,256]{2,1,0:T(8,128)} %copy-done.2, f32[1,256,256]{2,1,0:T(8,128)S(1)} %collective-permute-done.16), kind=kLoop, calls=%fused_computation.1 | loop fusion | flops 131072 | bytes 1048576 | tf_op jit(solution)/shard_map/concatenate | solution.py:318
  38.8 1.6 %collective-permute-start.5 = (f32[4,128,256]{2,1,0:T(8,128)}, f32[4,128,256]{2,1,0:T(8,128)}, u32[]{:S(2)}, u32[]{:S(2)}) collective-permute-start(f32[4,128,256]{2,1,0:T(8,128)} %collective-permute-done.3.refs_2_), channel_id=1, source_target_pairs={{0,1},{1,0},{2,3},{3,2},{4,5},{5,4},{6,7},{7,6},{8,9},{9,8},{10,11... | collective-permute-start | bytes 1572872 | tf_op jit(solution)/shard_map/ppermute | solution.py:264
  41.2 4.8 %collective-permute-done.4.refs_3_ = f32[4,128,256]{2,1,0:T(8,128)} collective-permute-done((f32[4,128,256]{2,1,0:T(8,128)S(1)}, f32[4,128,256]{2,1,0:T(8,128)}, u32[]{:S(2)}, u32[]{:S(2)}) %collective-permute-start.4) | collective-permute-done | bytes 524320 | tf_op jit(solution)/shard_map/ppermute | solution.py:264
  48.6 3.0 %dress.2 = (f32[4,128,256]{2,1,0:T(8,128)}, f32[4,128,256]{2,1,0:T(8,128)}) custom-call(s32[4]{0:T(128)} %pad_add_fusion.info, f32[16,16]{1,0:T(8,128)} %fusion.4.couplings, f32[4,256,256]{2,1,0:T(8,128)} %bitcast.28, f32[4,256,256]{2,1,0:T(8,128)} %copy-done.1), custom_call_target="tpu_custom_call" | custom-call | flops 4194304 | bytes 4194304 | tf_op jit(solution)/shard_map/dress/pallas_call | solution.py:62
  52.7 3.3 %dress.3 = (f32[4,128,256]{2,1,0:T(8,128)}, f32[4,128,256]{2,1,0:T(8,128)}) custom-call(s32[4]{0:T(128)} %pad_add_fusion.info, f32[16,16]{1,0:T(8,128)} %fusion.4.couplings, f32[4,256,256]{2,1,0:T(8,128)} %collective-permute-done.refs_0_, f32[4,256,256]{2,1,0:T(8,128)} %collective-permute-done.1.refs_1_, f32[4,128,256]{2,1,0:T(8,128)} %get-tuple-element.20.refs_2_, ...), custom_call_target="tpu_custom_call" | custom-call | flops 4194304 | bytes 4194304 | tf_op jit(solution)/shard_map/dress/pallas_call | solution.py:62
  56.0 14.2 %collective-permute-start.13 = (f32[4,128,256]{2,1,0:T(8,128)}, f32[4,128,256]{2,1,0:T(8,128)S(1)}, u32[]{:S(2)}, u32[]{:S(2)}) collective-permute-start(f32[4,128,256]{2,1,0:T(8,128)} %get-tuple-element.22.refs_0_.refs_5_), channel_id=1, source_target_pairs={{0,2},{1,3},{2,0},{3,1},{4,6},{5,7},{6,4},{7,5},{8,10},{9,11},{10,... | collective-permute-start | bytes 1572872 | tf_op jit(solution)/shard_map/ppermute | solution.py:264
  73.7 5.6 %pair.4 = (f32[2,4,64,128]{3,2,1,0:T(8,128)}, f32[2,4,64,128]{3,2,1,0:T(8,128)}) custom-call(s32[4]{0:T(128)} %pad_add_fusion.info, s32[8]{0:T(128)} %left_tiles.7, s32[8]{0:T(128)} %right_tiles.7, f32[4,128,256]{2,1,0:T(8,128)} %get-tuple-element.22.refs_0_.refs_5_, f32[4,128,256]{2,1,0:T(8,128)} %get-tuple-element.23.refs_1_.refs_6_, ...), custom_call_target="tpu_custom_call" | custom-call | flops 1610612736 | bytes 3145728 | tf_op jit(solution)/shard_map/pair/pallas_call | solution.py:192
  80.2 5.6 %pair.5 = (f32[2,3,64,128]{3,2,1,0:T(8,128)}, f32[2,3,64,128]{3,2,1,0:T(8,128)}) custom-call(s32[4]{0:T(128)} %pad_add_fusion.info, s32[8]{0:T(128)} %left_tiles.7, s32[8]{0:T(128)} %right_tiles.7, f32[4,128,256]{2,1,0:T(8,128)} %get-tuple-element.22.refs_0_.refs_5_, f32[4,128,256]{2,1,0:T(8,128)} %get-tuple-element.23.refs_1_.refs_6_, ...), custom_call_target="tpu_custom_call" | custom-call | flops 1610612736 | bytes 2621440 | tf_op jit(solution)/shard_map/pair/pallas_call | solution.py:192
  87.1 6.5 %collective-permute-done.14.refs_1_ = f32[4,128,256]{2,1,0:T(8,128)} collective-permute-done((f32[4,128,256]{2,1,0:T(8,128)}, f32[4,128,256]{2,1,0:T(8,128)}, u32[]{:S(2)}, u32[]{:S(2)}) %collective-permute-start.14) | collective-permute-done | bytes 524320 | tf_op jit(solution)/shard_map/ppermute | solution.py:264
  93.6 5.6 %pair.6 = (f32[2,3,64,128]{3,2,1,0:T(8,128)}, f32[2,3,64,128]{3,2,1,0:T(8,128)}) custom-call(s32[4]{0:T(128)} %pad_add_fusion.info, s32[8]{0:T(128)} %left_tiles.7, s32[8]{0:T(128)} %right_tiles.7, f32[4,128,256]{2,1,0:T(8,128)} %copy-done.7, f32[4,128,256]{2,1,0:T(8,128)} %collective-permute-done.14.refs_1_, f32[4,128,256]{2,1,0:T(8,128)} %copy-done.5, ...), custom_call_target="tpu_custom_call" | custom-call | flops 1610612736 | bytes 3145728 | tf_op jit(solution)/shard_map/pair/pallas_call | solution.py:192
  99.3 7.2 %pair.7 = (f32[2,6,64,128]{3,2,1,0:T(8,128)}, f32[2,6,64,128]{3,2,1,0:T(8,128)}) custom-call(s32[4]{0:T(128)} %pad_add_fusion.info, s32[8]{0:T(128)} %left_tiles.7, s32[8]{0:T(128)} %right_tiles.7, f32[4,128,256]{2,1,0:T(8,128)} %copy-done.7, f32[4,128,256]{2,1,0:T(8,128)} %collective-permute-done.14.refs_1_, f32[4,128,256]{2,1,0:T(8,128)} %collective-permute-done.3.refs_2_, ...), custom_call_target="tpu_custom_call" | custom-call | flops 2415919104 | bytes 4194304 | tf_op jit(solution)/shard_map/pair/pallas_call | solution.py:192
  110.6 1.5 %collective-permute-start.22 = (f32[1,6,64,128]{3,2,1,0:T(8,128)S(1)}, f32[1,6,64,128]{3,2,1,0:T(8,128)S(1)}, u32[]{:S(2)}, u32[]{:S(2)}) collective-permute-start(f32[1,6,64,128]{3,2,1,0:T(8,128)S(1)} %slice.89), channel_id=1, source_target_pairs={{0,16},{8,24},{16,0},{24,8},{1,17},{9,25},{17,1},{25,9},{2,18},{10... | collective-permute-start | bytes 589832 | tf_op jit(solution)/shard_map/ppermute | solution.py:254
  112.1 6.2 %collective-permute-done.20 = f32[1,3,64,128]{3,2,1,0:T(8,128)S(1)} collective-permute-done((f32[1,3,64,128]{3,2,1,0:T(8,128)S(1)}, f32[1,3,64,128]{3,2,1,0:T(8,128)S(1)}, u32[]{:S(2)}, u32[]{:S(2)}) %collective-permute-start.20) | collective-permute-done | bytes 98336 | tf_op jit(solution)/shard_map/ppermute | solution.py:254
  118.3 12.1 %collective-permute-start.24 = (f32[2,64,128]{2,1,0:T(8,128)S(1)}, f32[2,64,128]{2,1,0:T(8,128)S(1)}, u32[]{:S(2)}, u32[]{:S(2)}) collective-permute-start(f32[2,64,128]{2,1,0:T(8,128)S(1)} %fusion.3), channel_id=1, source_target_pairs={{0,2},{1,3},{2,0},{3,1},{4,6},{5,7},{6,4},{7,5},{8,10},{9,11},{10,... | collective-permute-start | bytes 196616 | tf_op jit(solution)/shard_map/ppermute | solution.py:264
  130.5 3.4 %collective-permute-start.23 = (f32[6,64,128]{2,1,0:T(8,128)S(1)}, f32[6,64,128]{2,1,0:T(8,128)S(1)}, u32[]{:S(2)}, u32[]{:S(2)}) collective-permute-start(f32[6,64,128]{2,1,0:T(8,128)S(1)} %fusion.2), channel_id=1, source_target_pairs={{0,2},{1,3},{2,0},{3,1},{4,6},{5,7},{6,4},{7,5},{8,10},{9,11},{10,... | collective-permute-start | bytes 589832 | tf_op jit(solution)/shard_map/ppermute | solution.py:264
  134.5 3.7 %collective-permute-done.23.refs_4_ = f32[6,64,128]{2,1,0:T(8,128)S(1)} collective-permute-done((f32[6,64,128]{2,1,0:T(8,128)S(1)}, f32[6,64,128]{2,1,0:T(8,128)S(1)}, u32[]{:S(2)}, u32[]{:S(2)}) %collective-permute-start.23) | collective-permute-done | bytes 196640 | tf_op jit(solution)/shard_map/ppermute | solution.py:264
  138.9 2.0 %finish.1 = f32[1,8,64,256]{3,2,1,0:T(8,128)} custom-call(s32[4]{0:T(128)} %pad_add_fusion.info, f32[7,64,128]{2,1,0:T(8,128)} %get-tuple-element.40.refs_0_, f32[7,64,128]{2,1,0:T(8,128)} %bitcast.31, f32[1,64,128]{2,1,0:T(8,128)} %slice_bitcast_fusion.1.refs_2_, f32[1,64,128]{2,1,0:T(8,128)} %slice_bitcast_fusion.refs_3_, f32[6,64,128]{2,1,0:T(8,128)} %copy-done.11, ...), custom_call_target="tpu_custom_call" | custom-call | flops 131072 | bytes 1048576 | tf_op jit(solution)/shard_map/finish/pallas_call | solution.py:229
  (88 shorter events, 23.3 us)
Async XLA Ops:
  0.0 27.4 %collective-permute-start = (f32[4,256,256]{2,1,0:T(8,128)}, f32[4,256,256]{2,1,0:T(8,128)}, u32[]{:S(2)}, u32[]{:S(2)}) collective-permute-start(f32[4,256,256]{2,1,0:T(8,128)} %bitcast.27), channel_id=1, source_target_pairs={{0,16},{8,24},{16,0},{24,8},{1,17},{9,25},{17,1},{25,9},{2,18},{10... | collective-permute-start | bytes 3145736 | tf_op jit(solution)/shard_map/ppermute | solution.py:254
  4.4 14.1 %collective-permute-start.8 = (f32[4,128,256]{2,1,0:T(8,128)S(1)}, f32[4,128,256]{2,1,0:T(8,128)}, u32[]{:S(2)}, u32[]{:S(2)}) collective-permute-start(f32[4,128,256]{2,1,0:T(8,128)S(1)} %get-tuple-element.24), channel_id=1, source_target_pairs={{2,4},{3,5},{4,2},{5,3},{10,12},{11,13},{12,10},{13,11},{18,20},{1... | collective-permute-start | bytes 1572872 | tf_op jit(solution)/shard_map/ppermute | solution.py:264
  6.8 9.5 %collective-permute-start.16 = (f32[1,256,256]{2,1,0:T(8,128)S(1)}, f32[1,256,256]{2,1,0:T(8,128)S(1)}, u32[]{:S(2)}, u32[]{:S(2)}) collective-permute-start(f32[1,256,256]{2,1,0:T(8,128)S(1)} %dynamic-slice_bitcast_fusion), channel_id=1, source_target_pairs={{0,2},{1,3},{2,0},{3,1},{4,6},{5,7},{6,4},{7,5},{8,10},{9,11},{10,... | collective-permute-start | bytes 786440 | tf_op jit(solution)/shard_map/ppermute | solution.py:264
  16.3 15.8 %collective-permute-start.17 = (f32[1,256,256]{2,1,0:T(8,128)S(1)}, f32[1,256,256]{2,1,0:T(8,128)S(1)}, u32[]{:S(2)}, u32[]{:S(2)}) collective-permute-start(f32[1,256,256]{2,1,0:T(8,128)S(1)} %collective-permute-done.16), channel_id=1, source_target_pairs={{0,16},{8,24},{16,0},{24,8},{1,17},{9,25},{17,1},{25,9},{2,18},{10... | collective-permute-start | bytes 786440 | tf_op jit(solution)/shard_map/ppermute | solution.py:254
  16.8 30.8 %collective-permute-start.2 = (f32[4,256,256]{2,1,0:T(8,128)S(1)}, f32[4,256,256]{2,1,0:T(8,128)S(1)}, u32[]{:S(2)}, u32[]{:S(2)}) collective-permute-start(f32[4,256,256]{2,1,0:T(8,128)S(1)} %bitcast.29), channel_id=1, source_target_pairs={{0,8},{8,0},{16,24},{24,16},{1,9},{9,1},{17,25},{25,17},{2,10},{10... | collective-permute-start | bytes 3145736 | tf_op jit(solution)/shard_map/ppermute | solution.py:254
  16.8 22.0 %collective-permute-start.3 = (f32[4,128,256]{2,1,0:T(8,128)S(1)}, f32[4,128,256]{2,1,0:T(8,128)}, u32[]{:S(2)}, u32[]{:S(2)}) collective-permute-start(f32[4,128,256]{2,1,0:T(8,128)S(1)} %get-tuple-element.24), channel_id=1, source_target_pairs={{0,4},{1,5},{2,0},{3,1},{4,6},{5,7},{6,2},{7,3},{8,12},{9,13},{10,... | collective-permute-start | bytes 1572872 | tf_op jit(solution)/shard_map/ppermute | solution.py:264
  18.5 20.3 %collective-permute-start.9 = (f32[4,128,256]{2,1,0:T(8,128)S(1)}, f32[4,128,256]{2,1,0:T(8,128)}, u32[]{:S(2)}, u32[]{:S(2)}) collective-permute-start(f32[4,128,256]{2,1,0:T(8,128)S(1)} %get-tuple-element.25), channel_id=1, source_target_pairs={{2,4},{3,5},{4,2},{5,3},{10,12},{11,13},{12,10},{13,11},{18,20},{1... | collective-permute-start | bytes 1572872 | tf_op jit(solution)/shard_map/ppermute | solution.py:264
  27.4 24.2 %collective-permute-start.1 = (f32[4,256,256]{2,1,0:T(8,128)}, f32[4,256,256]{2,1,0:T(8,128)}, u32[]{:S(2)}, u32[]{:S(2)}) collective-permute-start(f32[4,256,256]{2,1,0:T(8,128)} %collective-permute-done.refs_0_), channel_id=1, source_target_pairs={{0,8},{8,0},{16,24},{24,16},{1,9},{9,1},{17,25},{25,17},{2,10},{10... | collective-permute-start | bytes 3145736 | tf_op jit(solution)/shard_map/ppermute | solution.py:254
  32.8 13.3 %collective-permute-start.4 = (f32[4,128,256]{2,1,0:T(8,128)S(1)}, f32[4,128,256]{2,1,0:T(8,128)}, u32[]{:S(2)}, u32[]{:S(2)}) collective-permute-start(f32[4,128,256]{2,1,0:T(8,128)S(1)} %get-tuple-element.25), channel_id=1, source_target_pairs={{0,4},{1,5},{2,0},{3,1},{4,6},{5,7},{6,2},{7,3},{8,12},{9,13},{10,... | collective-permute-start | bytes 1572872 | tf_op jit(solution)/shard_map/ppermute | solution.py:264
  38.8 17.2 %collective-permute-start.18 = (f32[2,256,256]{2,1,0:T(8,128)}, f32[2,256,256]{2,1,0:T(8,128)}, u32[]{:S(2)}, u32[]{:S(2)}) collective-permute-start(f32[2,256,256]{2,1,0:T(8,128)} %pad_maximum_fusion.1), channel_id=1, source_target_pairs={{0,8},{8,0},{16,24},{24,16},{1,9},{9,1},{17,25},{25,17},{2,10},{10... | collective-permute-start | bytes 1572872 | tf_op jit(solution)/shard_map/ppermute | solution.py:254
  38.8 31.5 %collective-permute-start.5 = (f32[4,128,256]{2,1,0:T(8,128)}, f32[4,128,256]{2,1,0:T(8,128)}, u32[]{:S(2)}, u32[]{:S(2)}) collective-permute-start(f32[4,128,256]{2,1,0:T(8,128)} %collective-permute-done.3.refs_2_), channel_id=1, source_target_pairs={{0,1},{1,0},{2,3},{3,2},{4,5},{5,4},{6,7},{7,6},{8,9},{9,8},{10,11... | collective-permute-start | bytes 1572872 | tf_op jit(solution)/shard_map/ppermute | solution.py:264
  46.1 27.6 %collective-permute-start.6 = (f32[4,128,256]{2,1,0:T(8,128)}, f32[4,128,256]{2,1,0:T(8,128)}, u32[]{:S(2)}, u32[]{:S(2)}) collective-permute-start(f32[4,128,256]{2,1,0:T(8,128)} %collective-permute-done.4.refs_3_), channel_id=1, source_target_pairs={{0,1},{1,0},{2,3},{3,2},{4,5},{5,4},{6,7},{7,6},{8,9},{9,8},{10,11... | collective-permute-start | bytes 1572872 | tf_op jit(solution)/shard_map/ppermute | solution.py:264
  47.6 31.8 %collective-permute-start.10 = (f32[4,128,256]{2,1,0:T(8,128)}, f32[4,128,256]{2,1,0:T(8,128)S(1)}, u32[]{:S(2)}, u32[]{:S(2)}) collective-permute-start(f32[4,128,256]{2,1,0:T(8,128)} %broadcast_select_fusion.1.refs_2_.refs_6_), channel_id=1, source_target_pairs={{0,1},{1,0},{2,3},{3,2},{4,5},{5,4},{6,7},{7,6},{8,9},{9,8},{10,11... | collective-permute-start | bytes 1572872 | tf_op jit(solution)/shard_map/ppermute | solution.py:264
  51.6 35.4 %collective-permute-start.15 = (f32[4,128,256]{2,1,0:T(8,128)S(1)}, f32[4,128,256]{2,1,0:T(8,128)S(1)}, u32[]{:S(2)}, u32[]{:S(2)}) collective-permute-start(f32[4,128,256]{2,1,0:T(8,128)S(1)} %broadcast_select_fusion.refs_3_.refs_7_), channel_id=1, source_target_pairs={{0,1},{1,0},{2,3},{3,2},{4,5},{5,4},{6,7},{7,6},{8,9},{9,8},{10,11... | collective-permute-start | bytes 1572872 | tf_op jit(solution)/shard_map/ppermute | solution.py:264
  56.0 31.0 %collective-permute-start.13 = (f32[4,128,256]{2,1,0:T(8,128)}, f32[4,128,256]{2,1,0:T(8,128)S(1)}, u32[]{:S(2)}, u32[]{:S(2)}) collective-permute-start(f32[4,128,256]{2,1,0:T(8,128)} %get-tuple-element.22.refs_0_.refs_5_), channel_id=1, source_target_pairs={{0,2},{1,3},{2,0},{3,1},{4,6},{5,7},{6,4},{7,5},{8,10},{9,11},{10,... | collective-permute-start | bytes 1572872 | tf_op jit(solution)/shard_map/ppermute | solution.py:264
  70.3 23.3 %collective-permute-start.14 = (f32[4,128,256]{2,1,0:T(8,128)}, f32[4,128,256]{2,1,0:T(8,128)}, u32[]{:S(2)}, u32[]{:S(2)}) collective-permute-start(f32[4,128,256]{2,1,0:T(8,128)} %get-tuple-element.23.refs_1_.refs_6_), channel_id=1, source_target_pairs={{0,2},{1,3},{2,0},{3,1},{4,6},{5,7},{6,4},{7,5},{8,10},{9,11},{10,... | collective-permute-start | bytes 1572872 | tf_op jit(solution)/shard_map/ppermute | solution.py:264
  79.3 27.6 %collective-permute-start.7 = (f32[2,4,64,128]{3,2,1,0:T(8,128)}, f32[2,4,64,128]{3,2,1,0:T(8,128)S(1)}, u32[]{:S(2)}, u32[]{:S(2)}) collective-permute-start(f32[2,4,64,128]{3,2,1,0:T(8,128)} %get-tuple-element.27), channel_id=1, source_target_pairs={{0,8},{8,0},{16,24},{24,16},{1,9},{9,1},{17,25},{25,17},{2,10},{10... | collective-permute-start | bytes 786440 | tf_op jit(solution)/shard_map/ppermute | solution.py:254
  85.8 21.1 %collective-permute-start.11 = (f32[2,3,64,128]{3,2,1,0:T(8,128)}, f32[2,3,64,128]{3,2,1,0:T(8,128)S(1)}, u32[]{:S(2)}, u32[]{:S(2)}) collective-permute-start(f32[2,3,64,128]{3,2,1,0:T(8,128)} %get-tuple-element.30), channel_id=1, source_target_pairs={{0,8},{8,0},{16,24},{24,16},{1,9},{9,1},{17,25},{25,17},{2,10},{10... | collective-permute-start | bytes 589832 | tf_op jit(solution)/shard_map/ppermute | solution.py:254
  99.2 10.0 %collective-permute-start.19 = (f32[2,3,64,128]{3,2,1,0:T(8,128)}, f32[2,3,64,128]{3,2,1,0:T(8,128)S(1)}, u32[]{:S(2)}, u32[]{:S(2)}) collective-permute-start(f32[2,3,64,128]{3,2,1,0:T(8,128)} %get-tuple-element.32), channel_id=1, source_target_pairs={{0,8},{8,0},{16,24},{24,16},{1,9},{9,1},{17,25},{25,17},{2,10},{10... | collective-permute-start | bytes 589832 | tf_op jit(solution)/shard_map/ppermute | solution.py:254
  107.7 26.7 %collective-permute-start.12 = (f32[1,7,64,128]{3,2,1,0:T(8,128)S(1)}, f32[1,7,64,128]{3,2,1,0:T(8,128)S(1)}, u32[]{:S(2)}, u32[]{:S(2)}) collective-permute-start(f32[1,7,64,128]{3,2,1,0:T(8,128)S(1)} %get-tuple-element.39), channel_id=1, source_target_pairs={{0,16},{8,24},{16,0},{24,8},{1,17},{9,25},{17,1},{25,9},{2,18},{10... | collective-permute-start | bytes 688136 | tf_op jit(solution)/shard_map/ppermute | solution.py:254
  109.2 9.1 %collective-permute-start.20 = (f32[1,3,64,128]{3,2,1,0:T(8,128)S(1)}, f32[1,3,64,128]{3,2,1,0:T(8,128)S(1)}, u32[]{:S(2)}, u32[]{:S(2)}) collective-permute-start(f32[1,3,64,128]{3,2,1,0:T(8,128)S(1)} %slice.86), channel_id=1, source_target_pairs={{0,16},{8,24},{16,0},{24,8},{1,17},{9,25},{17,1},{25,9},{2,18},{10... | collective-permute-start | bytes 294920 | tf_op jit(solution)/shard_map/ppermute | solution.py:254
  110.6 19.9 %collective-permute-start.22 = (f32[1,6,64,128]{3,2,1,0:T(8,128)S(1)}, f32[1,6,64,128]{3,2,1,0:T(8,128)S(1)}, u32[]{:S(2)}, u32[]{:S(2)}) collective-permute-start(f32[1,6,64,128]{3,2,1,0:T(8,128)S(1)} %slice.89), channel_id=1, source_target_pairs={{0,16},{8,24},{16,0},{24,8},{1,17},{9,25},{17,1},{25,9},{2,18},{10... | collective-permute-start | bytes 589832 | tf_op jit(solution)/shard_map/ppermute | solution.py:254
  118.3 16.2 %collective-permute-start.24 = (f32[2,64,128]{2,1,0:T(8,128)S(1)}, f32[2,64,128]{2,1,0:T(8,128)S(1)}, u32[]{:S(2)}, u32[]{:S(2)}) collective-permute-start(f32[2,64,128]{2,1,0:T(8,128)S(1)} %fusion.3), channel_id=1, source_target_pairs={{0,2},{1,3},{2,0},{3,1},{4,6},{5,7},{6,4},{7,5},{8,10},{9,11},{10,... | collective-permute-start | bytes 196616 | tf_op jit(solution)/shard_map/ppermute | solution.py:264
  130.5 7.7 %collective-permute-start.23 = (f32[6,64,128]{2,1,0:T(8,128)S(1)}, f32[6,64,128]{2,1,0:T(8,128)S(1)}, u32[]{:S(2)}, u32[]{:S(2)}) collective-permute-start(f32[6,64,128]{2,1,0:T(8,128)S(1)} %fusion.2), channel_id=1, source_target_pairs={{0,2},{1,3},{2,0},{3,1},{4,6},{5,7},{6,4},{7,5},{8,10},{9,11},{10,... | collective-permute-start | bytes 589832 | tf_op jit(solution)/shard_map/ppermute | solution.py:264
  (18 other events, 181.3 us)

commit v2 on v1

--- a/solution.py
+++ b/solution.py
@@ -12,12 +12,16 @@
 BF16 = jnp.bfloat16
 VMEM = pl.BlockSpec(memory_space=pltpu.VMEM)
 SMEM = pl.BlockSpec(memory_space=pltpu.SMEM)
-ANY = pl.BlockSpec(memory_space=pl.ANY)
 
 
 def split(value):
     high = value.astype(BF16)
     return high, (value - high.astype(F32)).astype(BF16)
+
+
+def grant(arrays, shapes):
+    size = 4 * sum(a.size for a in list(arrays) + list(shapes)) + (8 << 20)
+    return pltpu.CompilerParams(vmem_limit_bytes=min(size, 60 << 20))
 
 
 def product(left, right, dims):
@@ -64,6 +68,7 @@
         out_shape=[shape, shape],
         in_specs=[SMEM, SMEM] + [VMEM] * (len(parts) + len(before)),
         out_specs=[VMEM, VMEM],
+        compiler_params=grant(list(parts) + list(before), [shape, shape]),
         cost_estimate=pl.CostEstimate(
             flops=8 * parts[0].size * len(parts),
             bytes_accessed=4 * parts[0].size * (len(parts) + 2),
@@ -74,12 +79,10 @@
 
 
 def pair_kernel(spec, info, left_tiles, right_tiles, *refs):
-    rows, inner, n_in, jobs, kinds, slots = spec
-    ins, outs = refs[:n_in], dict(zip(kinds, refs[n_in : n_in + len(kinds)]))
-    held = refs[n_in + len(kinds) : -2]
-    thetas, sem = refs[-2], refs[-1]
+    rows, inner, n_in, jobs, kinds = spec
+    ins, outs = refs[:n_in], dict(zip(kinds, refs[n_in:]))
     row, high, low, x_at = info[0], info[1], info[2], info[3]
-    size = thetas.shape[-1]
+    size = ins[0].shape[-1]
     quarter = size // 4
     width = size // 2
     count = 2 * inner
@@ -89,50 +92,23 @@
     def local_of(k, s):
         return ((high + k) % 2) * inner + (x_at + inner - s) % inner
 
-    copies, theta_copies = {}, []
+    made = {kind: 0 for kind in kinds}
     for lefts, theta_at, relative, foreign, pieces in jobs:
-        for i in [i for i, _ in lefts]:
-            if i not in copies:
-                copies[i] = pltpu.make_async_copy(ins[i], held[slots[i]], sem.at[i])
-                copies[i].start()
-        for k, s, _, rights in pieces:
+        tile = left_tiles[(2 * high + (1 - low if foreign else low)) * inner + x_at]
+        depth = lax.broadcasted_iota(jnp.int32, (size, size), 0)
+        wide = lax.broadcasted_iota(jnp.int32, (size, size), 1)
+        for k, s, column, rights in pieces:
             local = local_of(k, s)
+            limit = quarter * right_tiles[low * count + local]
             if relative:
                 per = count // rows
                 place = ((local // per) ^ row) * per + local % per
             else:
                 place = low * count + local
-            n = len(theta_copies)
-            theta_copies.append(
-                pltpu.make_async_copy(ins[theta_at].at[place], thetas.at[n], sem.at[n_in + n])
-            )
-            theta_copies[n].start()
-            for i in rights:
-                if i not in copies:
-                    copies[i] = pltpu.make_async_copy(ins[i], held[slots[i]], sem.at[i])
-                    copies[i].start()
-    waited = set()
-
-    def ready(i):
-        if i not in waited:
-            copies[i].wait()
-            waited.add(i)
-        return held[slots[i]]
-
-    made = {kind: 0 for kind in kinds}
-    n = 0
-    for lefts, _, relative, foreign, pieces in jobs:
-        tile = left_tiles[(2 * high + (1 - low if foreign else low)) * inner + x_at]
-        depth = lax.broadcasted_iota(jnp.int32, (size, size), 0)
-        wide = lax.broadcasted_iota(jnp.int32, (size, size), 1)
-        for k, s, column, rights in pieces:
-            limit = quarter * right_tiles[low * count + local_of(k, s)]
-            left_refs = [ready(i) for i, _ in lefts]
-            theta_copies[n].wait()
+            left_refs = [ins[i] for i, _ in lefts]
             inside = jnp.logical_and(depth < quarter * tile, wide < limit)
-            masked = split(jnp.where(inside, thetas[n], 0.0))
-            n += 1
-            right_refs = [ready(i) for i in rights]
+            masked = split(jnp.where(inside, ins[theta_at][place], 0.0))
+            right_refs = [ins[i] for i in rights]
             part = left_refs[0].shape[1]
             columns = sum(r.shape[1] for r in right_refs)
             total = None
@@ -160,7 +136,6 @@
                     for w in range(columns // width):
                         outs[kind][j, made[kind] + w] = value[:, w * width : (w + 1) * width]
                 made[kind] += columns // width
-    assert len(waited) == len(copies)
 
 
 def pair_products(rows, inner, scalars, jobs):
@@ -173,33 +148,29 @@
         arrays.append(array)
         return len(arrays) - 1
 
-    compact, streamed = [], []
+    compact = []
     units = {}
-    flops, n_thetas = 0, 0
+    flops = 0
     size = jobs[0][1].shape[-1]
     for lefts, theta, relative, foreign, pieces in jobs:
         lefts_at = tuple((index(a), kind) for a, kind in lefts)
         pieces_at = tuple((k, s, c, tuple(index(r) for r in rights)) for k, s, c, rights in pieces)
         compact.append((lefts_at, index(theta), relative, foreign, pieces_at))
-        streamed += [i for i, _ in lefts_at] + [i for piece in pieces_at for i in piece[3]]
-        n_thetas += len(pieces)
         for _, kind in lefts:
             units[kind] = units.get(kind, 0) + sum(r.shape[1] for p in pieces for r in p[3]) // (size // 2)
         flops += 12 * len(lefts) * len(pieces) * lefts[0][0].size * size
-    streamed = sorted(set(streamed))
-    slots = {i: n for n, i in enumerate(streamed)}
     kinds = tuple(units)
+    shapes = [
+        jax.ShapeDtypeStruct((rows // 2, units[kind], size // rows, size // 2), F32) for kind in kinds
+    ]
     out = pl.pallas_call(
-        functools.partial(pair_kernel, (rows, inner, len(arrays), tuple(compact), kinds, slots)),
-        out_shape=[
-            jax.ShapeDtypeStruct((rows // 2, units[kind], size // rows, size // 2), F32) for kind in kinds
-        ],
-        in_specs=[SMEM] * 3 + [ANY] * len(arrays),
+        functools.partial(pair_kernel, (rows, inner, len(arrays), tuple(compact), kinds)),
+        out_shape=shapes,
+        in_specs=[SMEM] * 3 + [VMEM] * len(arrays),
         out_specs=[VMEM] * len(kinds),
-        scratch_shapes=[pltpu.VMEM(arrays[i].shape, F32) for i in streamed]
-        + [pltpu.VMEM((n_thetas, size, size), F32), pltpu.SemaphoreType.DMA((len(arrays) + n_thetas,))],
+        compiler_params=grant(arrays, shapes),
         cost_estimate=pl.CostEstimate(
-            flops=flops, bytes_accessed=4 * sum(arrays[i].size for i in streamed), transcendentals=0
+            flops=flops, bytes_accessed=4 * sum(a.size for a in arrays), transcendentals=0
         ),
         name="pair",
     )(*scalars, *arrays)
@@ -226,9 +197,11 @@
 def finish(inner, info, groups, slab, size):
     arrays = [a for _, terms, _ in groups for a in terms]
     units = tuple((foreign, len(terms), tuple(listed)) for foreign, terms, listed in groups)
+    shape = jax.ShapeDtypeStruct((1, 4 * inner, slab, size), F32)
     return pl.pallas_call(
         functools.partial(finish_kernel, inner, units),
-        out_shape=jax.ShapeDtypeStruct((1, 4 * inner, slab, size), F32),
+        out_shape=shape,
+        compiler_params=grant(arrays, [shape]),
         in_specs=[SMEM] + [VMEM] * len(arrays),
         out_specs=VMEM,
         cost_estimate=pl.CostEstimate(

time: 141 us -> 133 us (0.943)
  Pallas kernels: 32.4 us -> 17.8 us
  waiting for transfers between devices: 39.9 us -> 49.5 us
  local copies, waits for them, and re-layouts: 7.17 us -> 2.39 us
  starting transfers between devices: 55.2 us -> 59.4 us
  other arithmetic: 5.26 us -> 2.65 us
    pallas_call x4, Pallas kernels: 24 us -> 12.9 us  [pair_products(): pl.pallas_call(functools.partial(pair_kernel, (rows, inner, len(arrays),...]
    ppermute x13, waiting for transfers between devices: 21.5 us -> 30.6 us  [by_blk(): return lax.ppermute(value, 'blk', moves)]
    ppermute x13, starting transfers between devices: 46.8 us -> 51.1 us  [by_blk(): return lax.ppermute(value, 'blk', moves)]
    pallas_call x2, Pallas kernels: 6.27 us -> 3.5 us  [dress(): pl.pallas_call(functools.partial(dress_kernel, shifts, rows), out_shape=[...]
    unnamed x34 -> x18, local copies, waits for them, and re-layouts: 2.62 us -> 0.04 us
  transfers between devices with their start and end apart: 25 -> 25, of which waited for: 8 -> 9; matrix products, arithmetic and copies ran while one was open for 8% -> 4% of each run, Pallas kernels for 22% -> 12%
where the time goes in v2:
time: 133 us; the launch traced here: 132 us
  starting transfers between devices  59.4 us (45%)
  waiting for transfers between devices  49.5 us (37%)
  Pallas kernels  17.8 us (13%)
  other arithmetic  2.65 us (2%)
  local copies, waits for them, and re-layouts  2.39 us (2%)
    ppermute x13, starting transfers between devices, by_blk(): return lax.ppermute(value, 'blk', moves)  51.1 us
    ppermute x13, waiting for transfers between devices, by_blk(): return lax.ppermute(value, 'blk', moves)  30.6 us
    ppermute x12, waiting for transfers between devices, by_row(): return lax.ppermute(value, 'row', [(r, r ^ shift) for r in range(rows)])  19 us
    pallas_call x4, Pallas kernels, pair_products(): pl.pallas_call(functools.partial(pair_kernel, (rows, inner, len(arrays),...  12.9 us
    ppermute x12, starting transfers between devices, by_row(): return lax.ppermute(value, 'row', [(r, r ^ shift) for r in range(rows)])  8.34 us
    pallas_call x2, Pallas kernels, dress(): pl.pallas_call(functools.partial(dress_kernel, shifts, rows), out_shape=[...  3.5 us
  transfers between devices with their start and end apart: 25, of which 9 were waited for; matrix products, arithmetic and copies ran while one was open for 4% of the time, Pallas kernels for 12%

profile of v2, /device:TPU:0, one launch (start us, length us, event | category | flops | bytes accessed | tf_op | source)
XLA Modules:
  0.0 132.2 jit_solution(1105276345486238926)
XLA Ops:
  0.0 3.1 %collective-permute-start = (f32[4,256,256]{2,1,0:T(8,128)}, f32[4,256,256]{2,1,0:T(8,128)}, u32[]{:S(2)}, u32[]{:S(2)}) collective-permute-start(f32[4,256,256]{2,1,0:T(8,128)} %bitcast.27), channel_id=1, source_target_pairs={{0,16},{8,24},{16,0},{24,8},{1,17},{9,25},{17,1},{25,9},{2,18},{10... | collective-permute-start | bytes 3145736 | tf_op jit(solution)/shard_map/ppermute | solution.py:227
  3.1 2.3 %fusion.11 = (f32[4,128,256]{2,1,0:T(8,128)}, f32[4,128,256]{2,1,0:T(8,128)}) fusion(f32[4,256,256]{2,1,0:T(8,128)} %bitcast.31), kind=kLoop, calls=%fused_computation.28 | loop fusion | bytes 2097152 | tf_op jit(solution)/shard_map/slice | solution.py:246
  6.8 3.7 %collective-permute-start.16 = (f32[1,256,256]{2,1,0:T(8,128)S(1)}, f32[1,256,256]{2,1,0:T(8,128)S(1)}, u32[]{:S(2)}, u32[]{:S(2)}) collective-permute-start(f32[1,256,256]{2,1,0:T(8,128)S(1)} %dynamic-slice_bitcast_fusion), channel_id=1, source_target_pairs={{0,2},{1,3},{2,0},{3,1},{4,6},{5,7},{6,4},{7,5},{8,10},{9,11},{10,... | collective-permute-start | bytes 786440 | tf_op jit(solution)/shard_map/ppermute | solution.py:237
  10.5 5.7 %collective-permute-done.16 = f32[1,256,256]{2,1,0:T(8,128)S(1)} collective-permute-done((f32[1,256,256]{2,1,0:T(8,128)S(1)}, f32[1,256,256]{2,1,0:T(8,128)S(1)}, u32[]{:S(2)}, u32[]{:S(2)}) %collective-permute-start.16) | collective-permute-done | bytes 262176 | tf_op jit(solution)/shard_map/ppermute | solution.py:237
  16.9 1.6 %collective-permute-start.3 = (f32[4,128,256]{2,1,0:T(8,128)}, f32[4,128,256]{2,1,0:T(8,128)}, u32[]{:S(2)}, u32[]{:S(2)}) collective-permute-start(f32[4,128,256]{2,1,0:T(8,128)} %get-tuple-element.24), channel_id=1, source_target_pairs={{0,4},{1,5},{2,0},{3,1},{4,6},{5,7},{6,2},{7,3},{8,12},{9,13},{10,... | collective-permute-start | bytes 1572872 | tf_op jit(solution)/shard_map/ppermute | solution.py:237
  20.0 7.4 %collective-permute-done.refs_0_ = f32[4,256,256]{2,1,0:T(8,128)} collective-permute-done((f32[4,256,256]{2,1,0:T(8,128)}, f32[4,256,256]{2,1,0:T(8,128)}, u32[]{:S(2)}, u32[]{:S(2)}) %collective-permute-start) | collective-permute-done | bytes 1048608 | tf_op jit(solution)/shard_map/ppermute | solution.py:227
  27.4 4.6 %collective-permute-done.17 = f32[1,256,256]{2,1,0:T(8,128)S(1)} collective-permute-done((f32[1,256,256]{2,1,0:T(8,128)S(1)}, f32[1,256,256]{2,1,0:T(8,128)S(1)}, u32[]{:S(2)}, u32[]{:S(2)}) %collective-permute-start.17) | collective-permute-done | bytes 262176 | tf_op jit(solution)/shard_map/ppermute | solution.py:227
  32.1 5.3 %collective-permute-start.4 = (f32[4,128,256]{2,1,0:T(8,128)}, f32[4,128,256]{2,1,0:T(8,128)}, u32[]{:S(2)}, u32[]{:S(2)}) collective-permute-start(f32[4,128,256]{2,1,0:T(8,128)} %get-tuple-element.25), channel_id=1, source_target_pairs={{0,4},{1,5},{2,0},{3,1},{4,6},{5,7},{6,2},{7,3},{8,12},{9,13},{10,... | collective-permute-start | bytes 1572872 | tf_op jit(solution)/shard_map/ppermute | solution.py:237
  41.7 9.1 %collective-permute-done.4.refs_3_ = f32[4,128,256]{2,1,0:T(8,128)} collective-permute-done((f32[4,128,256]{2,1,0:T(8,128)}, f32[4,128,256]{2,1,0:T(8,128)}, u32[]{:S(2)}, u32[]{:S(2)}) %collective-permute-start.4) | collective-permute-done | bytes 524320 | tf_op jit(solution)/shard_map/ppermute | solution.py:237
  54.3 1.6 %collective-permute-start.15 = (f32[4,128,256]{2,1,0:T(8,128)S(1)}, f32[4,128,256]{2,1,0:T(8,128)S(1)}, u32[]{:S(2)}, u32[]{:S(2)}) collective-permute-start(f32[4,128,256]{2,1,0:T(8,128)S(1)} %broadcast_select_fusion.refs_3_.refs_7_), channel_id=1, source_target_pairs={{0,1},{1,0},{2,3},{3,2},{4,5},{5,4},{6,7},{7,6},{8,9},{9,8},{10,11... | collective-permute-start | bytes 1572872 | tf_op jit(solution)/shard_map/ppermute | solution.py:237
  55.8 2.2 %dress.3 = (f32[4,128,256]{2,1,0:T(8,128)S(1)}, f32[4,128,256]{2,1,0:T(8,128)S(1)}) custom-call(s32[4]{0:T(128)S(1)} %pad_add_fusion.info, f32[16,16]{1,0:T(8,128)S(1)} %fusion.4.couplings, f32[4,256,256]{2,1,0:T(8,128)} %collective-permute-done.refs_0_, f32[4,256,256]{2,1,0:T(8,128)} %collective-permute-done.1.refs_1_, ...), custom_call_target="tpu_custom_call" | custom-call | flops 4194304 | bytes 4194304 | tf_op jit(solution)/shard_map/dress/pallas_call | solution.py:66
  58.1 8.7 %collective-permute-start.13 = (f32[4,128,256]{2,1,0:T(8,128)S(1)}, f32[4,128,256]{2,1,0:T(8,128)S(1)}, u32[]{:S(2)}, u32[]{:S(2)}) collective-permute-start(f32[4,128,256]{2,1,0:T(8,128)S(1)} %get-tuple-element.22.refs_0_.refs_5_), channel_id=1, source_target_pairs={{0,2},{1,3},{2,0},{3,1},{4,6},{5,7},{6,4},{7,5},{8,10},{9,11},{10,... | collective-permute-start | bytes 1572872 | tf_op jit(solution)/shard_map/ppermute | solution.py:237
  66.8 4.9 %collective-permute-start.14 = (f32[4,128,256]{2,1,0:T(8,128)S(1)}, f32[4,128,256]{2,1,0:T(8,128)S(1)}, u32[]{:S(2)}, u32[]{:S(2)}) collective-permute-start(f32[4,128,256]{2,1,0:T(8,128)S(1)} %get-tuple-element.23.refs_1_.refs_6_), channel_id=1, source_target_pairs={{0,2},{1,3},{2,0},{3,1},{4,6},{5,7},{6,4},{7,5},{8,10},{9,11},{10,... | collective-permute-start | bytes 1572872 | tf_op jit(solution)/shard_map/ppermute | solution.py:237
  71.9 3.3 %pair.4 = (f32[2,4,64,128]{3,2,1,0:T(8,128)S(1)}, f32[2,4,64,128]{3,2,1,0:T(8,128)S(1)}) custom-call(s32[4]{0:T(128)S(1)} %pad_add_fusion.info, s32[8]{0:T(128)S(1)} %copy-done.2, s32[8]{0:T(128)S(1)} %copy-done.3, f32[4,128,256]{2,1,0:T(8,128)S(1)} %get-tuple-element.22.refs_0_.refs_5_, f32[4,128,256]{2,1,0:T(8,128)S(1)} %get-tuple-element.23.refs_1_.refs_6_, ...), custom_call_target="tpu_custom_call" | custom-call | flops 1610612736 | bytes 5242880 | tf_op jit(solution)/shard_map/pair/pallas_call | solution.py:166
  75.3 1.8 %collective-permute-done.10.refs_4_.refs_2_ = f32[4,128,256]{2,1,0:T(8,128)S(1)} collective-permute-done((f32[4,128,256]{2,1,0:T(8,128)S(1)}, f32[4,128,256]{2,1,0:T(8,128)S(1)}, u32[]{:S(2)}, u32[]{:S(2)}) %collective-permute-start.10) | collective-permute-done | bytes 524320 | tf_op jit(solution)/shard_map/ppermute | solution.py:237
  77.0 2.7 %pair.5 = (f32[2,3,64,128]{3,2,1,0:T(8,128)S(1)}, f32[2,3,64,128]{3,2,1,0:T(8,128)S(1)}) custom-call(s32[4]{0:T(128)S(1)} %pad_add_fusion.info, s32[8]{0:T(128)S(1)} %copy-done.2, s32[8]{0:T(128)S(1)} %copy-done.3, f32[4,128,256]{2,1,0:T(8,128)S(1)} %get-tuple-element.22.refs_0_.refs_5_, f32[4,128,256]{2,1,0:T(8,128)S(1)} %get-tuple-element.23.refs_1_.refs_6_, ...), custom_call_target="tpu_custom_call" | custom-call | flops 1610612736 | bytes 4718592 | tf_op jit(solution)/shard_map/pair/pallas_call | solution.py:166
  79.8 7.4 %collective-permute-done.15.refs_3_ = f32[4,128,256]{2,1,0:T(8,128)S(1)} collective-permute-done((f32[4,128,256]{2,1,0:T(8,128)S(1)}, f32[4,128,256]{2,1,0:T(8,128)S(1)}, u32[]{:S(2)}, u32[]{:S(2)}) %collective-permute-start.15) | collective-permute-done | bytes 524320 | tf_op jit(solution)/shard_map/ppermute | solution.py:237
  87.2 2.3 %collective-permute-done.14.refs_1_ = f32[4,128,256]{2,1,0:T(8,128)S(1)} collective-permute-done((f32[4,128,256]{2,1,0:T(8,128)S(1)}, f32[4,128,256]{2,1,0:T(8,128)S(1)}, u32[]{:S(2)}, u32[]{:S(2)}) %collective-permute-start.14) | collective-permute-done | bytes 524320 | tf_op jit(solution)/shard_map/ppermute | solution.py:237
  89.5 2.7 %pair.6 = (f32[2,3,64,128]{3,2,1,0:T(8,128)S(1)}, f32[2,3,64,128]{3,2,1,0:T(8,128)S(1)}) custom-call(s32[4]{0:T(128)S(1)} %pad_add_fusion.info, s32[8]{0:T(128)S(1)} %copy-done.2, s32[8]{0:T(128)S(1)} %copy-done.3, f32[4,128,256]{2,1,0:T(8,128)S(1)} %collective-permute-done.13.refs_0_, f32[4,128,256]{2,1,0:T(8,128)S(1)} %collective-permute-done.14.refs_1_, ...), custom_call_target="tpu_custom_call" | custom-call | flops 1610612736 | bytes 6291456 | tf_op jit(solution)/shard_map/pair/pallas_call | solution.py:166
  92.3 4.2 %pair.7 = (f32[2,6,64,128]{3,2,1,0:T(8,128)S(1)}, f32[2,6,64,128]{3,2,1,0:T(8,128)S(1)}) custom-call(s32[4]{0:T(128)S(1)} %pad_add_fusion.info, s32[8]{0:T(128)S(1)} %copy-done.2, s32[8]{0:T(128)S(1)} %copy-done.3, f32[4,128,256]{2,1,0:T(8,128)S(1)} %collective-permute-done.13.refs_0_, f32[4,128,256]{2,1,0:T(8,128)S(1)} %collective-permute-done.14.refs_1_, ...), custom_call_target="tpu_custom_call" | custom-call | flops 2415919104 | bytes 5242880 | tf_op jit(solution)/shard_map/pair/pallas_call | solution.py:166
  100.9 6.9 %collective-permute-done.20 = f32[1,3,64,128]{3,2,1,0:T(8,128)S(1)} collective-permute-done((f32[1,3,64,128]{3,2,1,0:T(8,128)S(1)}, f32[1,3,64,128]{3,2,1,0:T(8,128)S(1)}, u32[]{:S(2)}, u32[]{:S(2)}) %collective-permute-start.20) | collective-permute-done | bytes 98336 | tf_op jit(solution)/shard_map/ppermute | solution.py:227
  107.8 15.5 %collective-permute-start.24 = (f32[2,64,128]{2,1,0:T(8,128)S(1)}, f32[2,64,128]{2,1,0:T(8,128)S(1)}, u32[]{:S(2)}, u32[]{:S(2)}) collective-permute-start(f32[2,64,128]{2,1,0:T(8,128)S(1)} %fusion.3), channel_id=1, source_target_pairs={{0,2},{1,3},{2,0},{3,1},{4,6},{5,7},{6,4},{7,5},{8,10},{9,11},{10,... | collective-permute-start | bytes 196616 | tf_op jit(solution)/shard_map/ppermute | solution.py:237
  123.4 3.3 %collective-permute-start.23 = (f32[6,64,128]{2,1,0:T(8,128)S(1)}, f32[6,64,128]{2,1,0:T(8,128)S(1)}, u32[]{:S(2)}, u32[]{:S(2)}) collective-permute-start(f32[6,64,128]{2,1,0:T(8,128)S(1)} %fusion.2), channel_id=1, source_target_pairs={{0,2},{1,3},{2,0},{3,1},{4,6},{5,7},{6,4},{7,5},{8,10},{9,11},{10,... | collective-permute-start | bytes 589832 | tf_op jit(solution)/shard_map/ppermute | solution.py:237
  126.6 4.2 %collective-permute-done.23.refs_4_ = f32[6,64,128]{2,1,0:T(8,128)S(1)} collective-permute-done((f32[6,64,128]{2,1,0:T(8,128)S(1)}, f32[6,64,128]{2,1,0:T(8,128)S(1)}, u32[]{:S(2)}, u32[]{:S(2)}) %collective-permute-start.23) | collective-permute-done | bytes 196640 | tf_op jit(solution)/shard_map/ppermute | solution.py:237
  (72 shorter events, 17.5 us)
Async XLA Ops:
  0.0 27.4 %collective-permute-start = (f32[4,256,256]{2,1,0:T(8,128)}, f32[4,256,256]{2,1,0:T(8,128)}, u32[]{:S(2)}, u32[]{:S(2)}) collective-permute-start(f32[4,256,256]{2,1,0:T(8,128)} %bitcast.27), channel_id=1, source_target_pairs={{0,16},{8,24},{16,0},{24,8},{1,17},{9,25},{17,1},{25,9},{2,18},{10... | collective-permute-start | bytes 3145736 | tf_op jit(solution)/shard_map/ppermute | solution.py:227
  5.3 13.2 %collective-permute-start.8 = (f32[4,128,256]{2,1,0:T(8,128)}, f32[4,128,256]{2,1,0:T(8,128)}, u32[]{:S(2)}, u32[]{:S(2)}) collective-permute-start(f32[4,128,256]{2,1,0:T(8,128)} %get-tuple-element.24), channel_id=1, source_target_pairs={{2,4},{3,5},{4,2},{5,3},{10,12},{11,13},{12,10},{13,11},{18,20},{1... | collective-permute-start | bytes 1572872 | tf_op jit(solution)/shard_map/ppermute | solution.py:237
  6.8 9.5 %collective-permute-start.16 = (f32[1,256,256]{2,1,0:T(8,128)S(1)}, f32[1,256,256]{2,1,0:T(8,128)S(1)}, u32[]{:S(2)}, u32[]{:S(2)}) collective-permute-start(f32[1,256,256]{2,1,0:T(8,128)S(1)} %dynamic-slice_bitcast_fusion), channel_id=1, source_target_pairs={{0,2},{1,3},{2,0},{3,1},{4,6},{5,7},{6,4},{7,5},{8,10},{9,11},{10,... | collective-permute-start | bytes 786440 | tf_op jit(solution)/shard_map/ppermute | solution.py:237
  16.3 15.8 %collective-permute-start.17 = (f32[1,256,256]{2,1,0:T(8,128)S(1)}, f32[1,256,256]{2,1,0:T(8,128)S(1)}, u32[]{:S(2)}, u32[]{:S(2)}) collective-permute-start(f32[1,256,256]{2,1,0:T(8,128)S(1)} %collective-permute-done.16), channel_id=1, source_target_pairs={{0,16},{8,24},{16,0},{24,8},{1,17},{9,25},{17,1},{25,9},{2,18},{10... | collective-permute-start | bytes 786440 | tf_op jit(solution)/shard_map/ppermute | solution.py:227
  16.9 35.4 %collective-permute-start.2 = (f32[4,256,256]{2,1,0:T(8,128)}, f32[4,256,256]{2,1,0:T(8,128)S(1)}, u32[]{:S(2)}, u32[]{:S(2)}) collective-permute-start(f32[4,256,256]{2,1,0:T(8,128)} %bitcast.28), channel_id=1, source_target_pairs={{0,8},{8,0},{16,24},{24,16},{1,9},{9,1},{17,25},{25,17},{2,10},{10... | collective-permute-start | bytes 3145736 | tf_op jit(solution)/shard_map/ppermute | solution.py:227
  16.9 22.2 %collective-permute-start.3 = (f32[4,128,256]{2,1,0:T(8,128)}, f32[4,128,256]{2,1,0:T(8,128)}, u32[]{:S(2)}, u32[]{:S(2)}) collective-permute-start(f32[4,128,256]{2,1,0:T(8,128)} %get-tuple-element.24), channel_id=1, source_target_pairs={{0,4},{1,5},{2,0},{3,1},{4,6},{5,7},{6,2},{7,3},{8,12},{9,13},{10,... | collective-permute-start | bytes 1572872 | tf_op jit(solution)/shard_map/ppermute | solution.py:237
  18.6 20.2 %collective-permute-start.9 = (f32[4,128,256]{2,1,0:T(8,128)}, f32[4,128,256]{2,1,0:T(8,128)}, u32[]{:S(2)}, u32[]{:S(2)}) collective-permute-start(f32[4,128,256]{2,1,0:T(8,128)} %get-tuple-element.25), channel_id=1, source_target_pairs={{2,4},{3,5},{4,2},{5,3},{10,12},{11,13},{12,10},{13,11},{18,20},{1... | collective-permute-start | bytes 1572872 | tf_op jit(solution)/shard_map/ppermute | solution.py:237
  27.4 26.9 %collective-permute-start.1 = (f32[4,256,256]{2,1,0:T(8,128)}, f32[4,256,256]{2,1,0:T(8,128)}, u32[]{:S(2)}, u32[]{:S(2)}) collective-permute-start(f32[4,256,256]{2,1,0:T(8,128)} %collective-permute-done.refs_0_), channel_id=1, source_target_pairs={{0,8},{8,0},{16,24},{24,16},{1,9},{9,1},{17,25},{25,17},{2,10},{10... | collective-permute-start | bytes 3145736 | tf_op jit(solution)/shard_map/ppermute | solution.py:227
  32.1 18.7 %collective-permute-start.4 = (f32[4,128,256]{2,1,0:T(8,128)}, f32[4,128,256]{2,1,0:T(8,128)}, u32[]{:S(2)}, u32[]{:S(2)}) collective-permute-start(f32[4,128,256]{2,1,0:T(8,128)} %get-tuple-element.25), channel_id=1, source_target_pairs={{0,4},{1,5},{2,0},{3,1},{4,6},{5,7},{6,2},{7,3},{8,12},{9,13},{10,... | collective-permute-start | bytes 1572872 | tf_op jit(solution)/shard_map/ppermute | solution.py:237
  38.8 19.3 %collective-permute-start.18 = (f32[2,256,256]{2,1,0:T(8,128)S(1)}, f32[2,256,256]{2,1,0:T(8,128)S(1)}, u32[]{:S(2)}, u32[]{:S(2)}) collective-permute-start(f32[2,256,256]{2,1,0:T(8,128)S(1)} %pad_maximum_fusion.1), channel_id=1, source_target_pairs={{0,8},{8,0},{16,24},{24,16},{1,9},{9,1},{17,25},{25,17},{2,10},{10... | collective-permute-start | bytes 1572872 | tf_op jit(solution)/shard_map/ppermute | solution.py:227
  39.1 27.7 %collective-permute-start.5 = (f32[4,128,256]{2,1,0:T(8,128)}, f32[4,128,256]{2,1,0:T(8,128)S(1)}, u32[]{:S(2)}, u32[]{:S(2)}) collective-permute-start(f32[4,128,256]{2,1,0:T(8,128)} %collective-permute-done.3.refs_2_), channel_id=1, source_target_pairs={{0,1},{1,0},{2,3},{3,2},{4,5},{5,4},{6,7},{7,6},{8,9},{9,8},{10,11... | collective-permute-start | bytes 1572872 | tf_op jit(solution)/shard_map/ppermute | solution.py:237
  50.8 21.1 %collective-permute-start.6 = (f32[4,128,256]{2,1,0:T(8,128)}, f32[4,128,256]{2,1,0:T(8,128)S(1)}, u32[]{:S(2)}, u32[]{:S(2)}) collective-permute-start(f32[4,128,256]{2,1,0:T(8,128)} %collective-permute-done.4.refs_3_), channel_id=1, source_target_pairs={{0,1},{1,0},{2,3},{3,2},{4,5},{5,4},{6,7},{7,6},{8,9},{9,8},{10,11... | collective-permute-start | bytes 1572872 | tf_op jit(solution)/shard_map/ppermute | solution.py:237
  52.4 24.7 %collective-permute-start.10 = (f32[4,128,256]{2,1,0:T(8,128)S(1)}, f32[4,128,256]{2,1,0:T(8,128)S(1)}, u32[]{:S(2)}, u32[]{:S(2)}) collective-permute-start(f32[4,128,256]{2,1,0:T(8,128)S(1)} %broadcast_select_fusion.1.refs_2_.refs_6_), channel_id=1, source_target_pairs={{0,1},{1,0},{2,3},{3,2},{4,5},{5,4},{6,7},{7,6},{8,9},{9,8},{10,11... | collective-permute-start | bytes 1572872 | tf_op jit(solution)/shard_map/ppermute | solution.py:237
  54.3 32.9 %collective-permute-start.15 = (f32[4,128,256]{2,1,0:T(8,128)S(1)}, f32[4,128,256]{2,1,0:T(8,128)S(1)}, u32[]{:S(2)}, u32[]{:S(2)}) collective-permute-start(f32[4,128,256]{2,1,0:T(8,128)S(1)} %broadcast_select_fusion.refs_3_.refs_7_), channel_id=1, source_target_pairs={{0,1},{1,0},{2,3},{3,2},{4,5},{5,4},{6,7},{7,6},{8,9},{9,8},{10,11... | collective-permute-start | bytes 1572872 | tf_op jit(solution)/shard_map/ppermute | solution.py:237
  58.1 29.1 %collective-permute-start.13 = (f32[4,128,256]{2,1,0:T(8,128)S(1)}, f32[4,128,256]{2,1,0:T(8,128)S(1)}, u32[]{:S(2)}, u32[]{:S(2)}) collective-permute-start(f32[4,128,256]{2,1,0:T(8,128)S(1)} %get-tuple-element.22.refs_0_.refs_5_), channel_id=1, source_target_pairs={{0,2},{1,3},{2,0},{3,1},{4,6},{5,7},{6,4},{7,5},{8,10},{9,11},{10,... | collective-permute-start | bytes 1572872 | tf_op jit(solution)/shard_map/ppermute | solution.py:237
  66.8 22.7 %collective-permute-start.14 = (f32[4,128,256]{2,1,0:T(8,128)S(1)}, f32[4,128,256]{2,1,0:T(8,128)S(1)}, u32[]{:S(2)}, u32[]{:S(2)}) collective-permute-start(f32[4,128,256]{2,1,0:T(8,128)S(1)} %get-tuple-element.23.refs_1_.refs_6_), channel_id=1, source_target_pairs={{0,2},{1,3},{2,0},{3,1},{4,6},{5,7},{6,4},{7,5},{8,10},{9,11},{10,... | collective-permute-start | bytes 1572872 | tf_op jit(solution)/shard_map/ppermute | solution.py:237
  75.2 21.9 %collective-permute-start.7 = (f32[2,4,64,128]{3,2,1,0:T(8,128)S(1)}, f32[2,4,64,128]{3,2,1,0:T(8,128)S(1)}, u32[]{:S(2)}, u32[]{:S(2)}) collective-permute-start(f32[2,4,64,128]{3,2,1,0:T(8,128)S(1)} %get-tuple-element.27), channel_id=1, source_target_pairs={{0,8},{8,0},{16,24},{24,16},{1,9},{9,1},{17,25},{25,17},{2,10},{10... | collective-permute-start | bytes 786440 | tf_op jit(solution)/shard_map/ppermute | solution.py:227
  79.7 17.3 %collective-permute-start.11 = (f32[2,3,64,128]{3,2,1,0:T(8,128)S(1)}, f32[2,3,64,128]{3,2,1,0:T(8,128)S(1)}, u32[]{:S(2)}, u32[]{:S(2)}) collective-permute-start(f32[2,3,64,128]{3,2,1,0:T(8,128)S(1)} %get-tuple-element.30), channel_id=1, source_target_pairs={{0,8},{8,0},{16,24},{24,16},{1,9},{9,1},{17,25},{25,17},{2,10},{10... | collective-permute-start | bytes 589832 | tf_op jit(solution)/shard_map/ppermute | solution.py:227
  92.2 6.4 %collective-permute-start.19 = (f32[2,3,64,128]{3,2,1,0:T(8,128)S(1)}, f32[2,3,64,128]{3,2,1,0:T(8,128)S(1)}, u32[]{:S(2)}, u32[]{:S(2)}) collective-permute-start(f32[2,3,64,128]{3,2,1,0:T(8,128)S(1)} %get-tuple-element.32), channel_id=1, source_target_pairs={{0,8},{8,0},{16,24},{24,16},{1,9},{9,1},{17,25},{25,17},{2,10},{10... | collective-permute-start | bytes 589832 | tf_op jit(solution)/shard_map/ppermute | solution.py:227
  97.2 29.4 %collective-permute-start.12 = (f32[1,7,64,128]{3,2,1,0:T(8,128)S(1)}, f32[1,7,64,128]{3,2,1,0:T(8,128)S(1)}, u32[]{:S(2)}, u32[]{:S(2)}) collective-permute-start(f32[1,7,64,128]{3,2,1,0:T(8,128)S(1)} %get-tuple-element.39), channel_id=1, source_target_pairs={{0,16},{8,24},{16,0},{24,8},{1,17},{9,25},{17,1},{25,9},{2,18},{10... | collective-permute-start | bytes 688136 | tf_op jit(solution)/shard_map/ppermute | solution.py:227
  98.7 9.2 %collective-permute-start.20 = (f32[1,3,64,128]{3,2,1,0:T(8,128)S(1)}, f32[1,3,64,128]{3,2,1,0:T(8,128)S(1)}, u32[]{:S(2)}, u32[]{:S(2)}) collective-permute-start(f32[1,3,64,128]{3,2,1,0:T(8,128)S(1)} %slice.86), channel_id=1, source_target_pairs={{0,16},{8,24},{16,0},{24,8},{1,17},{9,25},{17,1},{25,9},{2,18},{10... | collective-permute-start | bytes 294920 | tf_op jit(solution)/shard_map/ppermute | solution.py:227
  99.5 23.9 %collective-permute-start.22 = (f32[1,6,64,128]{3,2,1,0:T(8,128)S(1)}, f32[1,6,64,128]{3,2,1,0:T(8,128)S(1)}, u32[]{:S(2)}, u32[]{:S(2)}) collective-permute-start(f32[1,6,64,128]{3,2,1,0:T(8,128)S(1)} %slice.89), channel_id=1, source_target_pairs={{0,16},{8,24},{16,0},{24,8},{1,17},{9,25},{17,1},{25,9},{2,18},{10... | collective-permute-start | bytes 589832 | tf_op jit(solution)/shard_map/ppermute | solution.py:227
  107.8 18.8 %collective-permute-start.24 = (f32[2,64,128]{2,1,0:T(8,128)S(1)}, f32[2,64,128]{2,1,0:T(8,128)S(1)}, u32[]{:S(2)}, u32[]{:S(2)}) collective-permute-start(f32[2,64,128]{2,1,0:T(8,128)S(1)} %fusion.3), channel_id=1, source_target_pairs={{0,2},{1,3},{2,0},{3,1},{4,6},{5,7},{6,4},{7,5},{8,10},{9,11},{10,... | collective-permute-start | bytes 196616 | tf_op jit(solution)/shard_map/ppermute | solution.py:237
  123.4 7.5 %collective-permute-start.23 = (f32[6,64,128]{2,1,0:T(8,128)S(1)}, f32[6,64,128]{2,1,0:T(8,128)S(1)}, u32[]{:S(2)}, u32[]{:S(2)}) collective-permute-start(f32[6,64,128]{2,1,0:T(8,128)S(1)} %fusion.2), channel_id=1, source_target_pairs={{0,2},{1,3},{2,0},{3,1},{4,6},{5,7},{6,4},{7,5},{8,10},{9,11},{10,... | collective-permute-start | bytes 589832 | tf_op jit(solution)/shard_map/ppermute | solution.py:237
  (10 other events, 153.2 us)
